TPU v7x, 32 devices: a whole 2x2x4 slice. The times are simulated.
32 devices in a mesh: seq: 16 (over z, x, core), kv: 2 (over y).
Axes of the slice: x: 2, y: 2, z: 4, core: 2. Of those that a mesh axis runs over, the one named last changes fastest.
Arguments:
- q_band: bfloat16 [4096, 4096], P('seq', 'kv'), may hold values from -10 to 10
- k_band: bfloat16 [4096, 512], P('seq', 'kv'), may hold values from -10 to 10
- v_band: bfloat16 [4096, 512], P('seq', 'kv'), may hold values from -6 to 6
- sink_band: float32 [64], P('kv'), may hold values from -1 to 3
- q_doc: bfloat16 [4096, 4096], P('seq', 'kv'), may hold values from -10 to 10
- k_doc: bfloat16 [4096, 512], P('seq', 'kv'), may hold values from -10 to 10
- v_doc: bfloat16 [4096, 512], P('seq', 'kv'), may hold values from -6 to 6
- sink_doc: float32 [64], P('kv'), may hold values from -1 to 3
- doc_starts: int32 [16], replicated, may hold values from 0 to 4095, as said below
- source_lists: int32 [16, 8], P('seq'), may hold values from -1 to 14, as said below
Outputs:
- out_band: bfloat16 [4096, 4096], P(('seq', 'kv'))
- out_doc: bfloat16 [4096, 4096], P(('seq', 'kv'))
Inputs may be any that keep to these rules, and one draw needn't show every extreme that they name: `doc_starts`: Non-decreasing, the first entry 0; equal neighbours mark empty documents; no document holds more than 2048 tokens and one holds exactly 2048. `source_lists`: row s names, in falling order, every earlier shard from s - 1 down to the shard in which the document holding shard s's first token begins; -1 fills the remaining entries. Some row names 8 shards.
All inputs are finite; a program needn't handle non-finite values.
Results may differ from a plain program's by a relative error of at most 0.0039.
Values may be sent and summed in bfloat16 or wider, within the bound.
No kernel may reach another device: no remote copies, remote signals or barrier semaphores. Data moves between devices by JAX's collectives and lax.ppermute only.
A program may use at most 64 MiB of HBM per device.

v0:
```python
import functools
import jax
import jax.numpy as jnp
from jax import lax
from jax.experimental import pallas as pl
from jax.experimental.pallas import tpu as pltpu
from jax.sharding import PartitionSpec as P

HD = 64
G = 8
WIN = 128
BACK = 8
LOG2E = 1.4426950408889634
SCORE_SCALE = HD ** (-0.5) * LOG2E
NEG = -1e30


def start_of(starts_ref, position):
    found = jnp.int32(0)
    for i in range(starts_ref.shape[0]):
        entry = starts_ref[i]
        found = jnp.where(entry <= position, jnp.maximum(found, entry), found)
    return found


def start_row(starts_ref, positions):
    found = jnp.zeros_like(positions)
    for i in range(starts_ref.shape[0]):
        entry = starts_ref[i]
        found = jnp.where(positions >= entry, jnp.maximum(found, entry), found)
    return found


def fold_in(state, key_block, query_cols, value_rows, kept):
    top, total, acc = state
    scores = jnp.dot(key_block, query_cols, preferred_element_type=jnp.float32)
    if kept is not None:
        scores = jnp.where(kept, scores, NEG)
    new_top = jnp.maximum(top, jnp.max(scores, axis=0, keepdims=True) * SCORE_SCALE)
    weight = jnp.exp2(scores * SCORE_SCALE - new_top)
    fading = jnp.exp2(top - new_top)
    total = total * fading + jnp.sum(weight, axis=0, keepdims=True)
    acc = acc * fading + jnp.dot(
        value_rows, weight.astype(jnp.bfloat16), preferred_element_type=jnp.float32
    )
    return new_top, total, acc


def slot_cols(query_cols, slot, slots):
    if slots == 1:
        return query_cols
    empty = jnp.zeros_like(query_cols)
    return jnp.concatenate([query_cols if i == slot else empty for i in range(slots)], axis=0)


def doc_body(plan, *refs):
    first, last, grp, heads, rows = plan.first, plan.last, plan.grp, plan.heads, plan.rows
    refs = list(refs)
    where_ref, starts_ref, list_ref, sink_ref = refs[:4]
    del refs[:4]
    mate_list_ref = refs.pop(0) if grp == 2 else None
    query_refs = [refs.pop(0) for _ in range(grp)]
    unit_refs = [refs.pop(0) for _ in range(plan.units)]
    if not first:
        acc_in, stat_in = refs.pop(0), refs.pop(0)
    if last:
        piece_refs = [refs.pop(0) for _ in range(2 * grp if plan.pieces else 1)]
    else:
        acc_out, stat_out = refs.pop(0), refs.pop(0)
    value_ref, start_ref, flag_ref, acc_ref, stat_ref = refs
    step = pl.program_id(0)
    pairs = G // 2
    own_shard = where_ref[0]
    shards = [own_shard, own_shard ^ 1][:grp]
    width = heads * HD
    blocks = [(n, r) for n in range(plan.units) for r in range(grp)]
    key_shards = []
    for n, r in blocks:
        key_shards.append(shards[r] - where_ref[4 + n])

    @pl.when(step == 0)
    def _():
        for n in range(plan.units):
            unit = unit_refs[n][...]
            if width % 128 == 0:
                value_ref[n] = unit[:, width:].T
            else:
                value_ref[n] = unit.T[width:]
        for a in range(grp):
            q_low = shards[a] * rows
            start_low = start_of(starts_ref, q_low)
            start_high = start_of(starts_ref, q_low + rows - 1)
            positions = q_low + lax.broadcasted_iota(jnp.int32, (8, rows), 1)
            start_ref[a] = start_row(starts_ref, positions)
            if a == 1:
                mate_row = mate_list_ref[...].astype(jnp.float32)[:1]
                lanes = lax.broadcasted_iota(jnp.int32, mate_row.shape, 1)
            for b, (n, r) in enumerate(blocks):
                shard = key_shards[b]
                if a == 0:
                    named = shard == shards[0]
                    for i in range(BACK):
                        named = named | (list_ref[0, i] == shard)
                else:
                    same = (mate_row == shard.astype(jnp.float32)) & (lanes < BACK)
                    named = (shard == shards[1]) | (jnp.max(same.astype(jnp.float32)) > 0.5)
                k_low = shard * rows
                live = named & (shard >= 0) & (shard <= shards[a]) & (k_low + rows > start_low)
                whole = (k_low >= start_high) & (shard < shards[a])
                flag_ref[a, b] = jnp.where(live, jnp.where(whole, 2, 1), 0)

    head = step // pairs
    for a in range(grp):
        span = slice(a * rows, (a + 1) * rows)
        if first:
            for e in range(2):
                sink = sink_ref[where_ref[1] * heads * G + 2 * step + e] * LOG2E
                stat_ref[e : e + 1, span] = jnp.full((1, rows), sink, jnp.float32)
            stat_ref[2:4, span] = jnp.ones((2, rows), jnp.float32)
            acc_ref[:, span] = jnp.zeros((2 * HD, rows), jnp.float32)
    if not first:
        acc_ref[...] = acc_in[0]
        stat_ref[...] = stat_in[0]

    value_span = pl.ds(pl.multiple_of(head * HD, HD), HD)
    for a in range(grp):
        span = slice(a * rows, (a + 1) * rows)
        turned = query_refs[a][...].T
        cols = []
        for e in range(2):
            col = turned[e * HD : (e + 1) * HD]
            if heads > 1:
                empty = jnp.zeros_like(col)
                col = jnp.concatenate(
                    [jnp.where(head == i, col, empty) for i in range(heads)], axis=0
                )
            cols.append(col)
        for b, (n, r) in enumerate(blocks):
            key_block = unit_refs[n].at[r * rows : (r + 1) * rows, :width]
            value_rows = value_ref.at[n, value_span, r * rows : (r + 1) * rows]

            def work(masked, a=a, b=b, span=span, key_block=key_block, value_rows=value_rows):
                kept = None
                if masked:
                    u = key_shards[b] * rows + lax.broadcasted_iota(jnp.int32, (rows, rows), 0)
                    t = shards[a] * rows + lax.broadcasted_iota(jnp.int32, (rows, rows), 1)
                    kept = (u <= t) & (u >= start_ref[a][:1])
                for e in range(2):
                    state = (
                        stat_ref[e : e + 1, span],
                        stat_ref[2 + e : 3 + e, span],
                        acc_ref[e * HD : (e + 1) * HD, span],
                    )
                    top, total, acc = fold_in(state, key_block[...], cols[e], value_rows[...], kept)
                    stat_ref[e : e + 1, span] = top
                    stat_ref[2 + e : 3 + e, span] = total
                    acc_ref[e * HD : (e + 1) * HD, span] = acc

            pl.when(flag_ref[a, b] == 1)(functools.partial(work, True))
            pl.when(flag_ref[a, b] == 2)(functools.partial(work, False))

    if not last:
        acc_out[0] = acc_ref[...]
        stat_out[0] = stat_ref[...]
        return
    for a in range(grp):
        span = slice(a * rows, (a + 1) * rows)
        parts = [
            acc_ref[e * HD : (e + 1) * HD, span] / stat_ref[2 + e : 3 + e, span] for e in range(2)
        ]
        result = jnp.concatenate(parts, axis=0).T.astype(jnp.bfloat16)
        if not plan.pieces:
            piece_refs[0][...] = result
            continue
        half = rows // 2
        side = where_ref[2]
        low, high = result[:half], result[half:]
        piece_refs[2 * a][...] = jnp.where(side == 0, low, high)
        piece_refs[2 * a + 1][...] = jnp.where(side == 0, high, low)


class DocPlan:
    def __init__(self, first, last, grp, heads, units, rows, pieces):
        self.first, self.last, self.grp, self.heads = first, last, grp, heads
        self.units, self.rows, self.pieces = units, rows, pieces


def doc_call(plan, where, starts, sources, sinks, mate_rows, queries, units, state, columns):
    grp, heads, rows = plan.grp, plan.heads, plan.rows
    steps = heads * G // 2
    width = heads * HD
    smem = pl.BlockSpec(memory_space=pltpu.SMEM)
    args = [where, starts, sources, sinks]
    specs = [smem, smem, smem]
    if grp == 2:
        args.append(mate_rows)
        specs.append(pl.BlockSpec((16, 128), lambda j, w: (rows // 16, 0)))
    args += list(queries)
    specs.append(pl.BlockSpec((rows, 128), lambda j, w: (0, w[1] * steps + j)))
    if grp == 2:
        specs.append(pl.BlockSpec((rows, 128), lambda j, w: (0, j)))
    for unit in units:
        args.append(unit)
        specs.append(pl.BlockSpec((grp * rows, 2 * width), lambda j, w: (0, 0)))
    lanes = grp * rows
    state_specs = [
        pl.BlockSpec((1, 2 * HD, lanes), lambda j, w: (j, 0, 0)),
        pl.BlockSpec((1, 8, lanes), lambda j, w: (j, 0, 0)),
    ]
    state_shapes = [
        jax.ShapeDtypeStruct((steps, 2 * HD, lanes), jnp.float32),
        jax.ShapeDtypeStruct((steps, 8, lanes), jnp.float32),
    ]
    aliases = {}
    if not plan.first:
        if not plan.last:
            aliases = {len(args): 0, len(args) + 1: 1}
        args += list(state)
        specs += state_specs
    if not plan.last:
        out_shape, out_specs = state_shapes, state_specs
    elif plan.pieces:
        half = rows // 2
        out_shape = [jax.ShapeDtypeStruct((half, columns), jnp.bfloat16)]
        out_specs = [pl.BlockSpec((half, 128), lambda j, w: (0, w[3] * steps + j))]
        for _ in range(2 * grp - 1):
            out_shape.append(jax.ShapeDtypeStruct((half, steps * 128), jnp.bfloat16))
            out_specs.append(pl.BlockSpec((half, 128), lambda j, w: (0, j)))
    else:
        out_shape = [jax.ShapeDtypeStruct((rows, steps * 128), jnp.bfloat16)]
        out_specs = [pl.BlockSpec((rows, 128), lambda j, w: (0, j))]
    blocks = grp * plan.units
    return pl.pallas_call(
        functools.partial(doc_body, plan),
        out_shape=out_shape,
        grid_spec=pltpu.PrefetchScalarGridSpec(
            num_scalar_prefetch=1,
            grid=(steps,),
            in_specs=specs,
            out_specs=out_specs,
            scratch_shapes=[
                pltpu.VMEM((plan.units, width, grp * rows), jnp.bfloat16),
                pltpu.VMEM((grp, 8, rows), jnp.int32),
                pltpu.SMEM((grp, blocks), jnp.int32),
                pltpu.VMEM((2 * HD, lanes), jnp.float32),
                pltpu.VMEM((8, lanes), jnp.float32),
            ],
        ),
        input_output_aliases=aliases,
        compiler_params=pltpu.CompilerParams(
            dimension_semantics=("arbitrary",), vmem_limit_bytes=48 * 1024 * 1024
        ),
        name="doc_attention",
    )(*args)


def band_body(heads, rows, pieces, where_ref, starts_ref, sink_ref, query_ref, key_ref, value_ref, rim_ref, *refs):
    out_refs, (keys, values, start_ref) = refs[:-3], refs[-3:]
    step = pl.program_id(0)
    width = heads * HD
    low = where_ref[0] * rows

    @pl.when(step == 0)
    def _():
        rim = rim_ref[...]
        keys[:WIN] = rim[:, :width]
        keys[WIN:] = key_ref[...]
        if width % 128 == 0:
            values[:, :WIN] = rim[:, width:].T
        else:
            values[:, :WIN] = rim.T[width:]
        values[:, WIN:] = value_ref[...].T
        positions = low + lax.broadcasted_iota(jnp.int32, (8, rows), 1)
        start_ref[...] = start_row(starts_ref, positions)

    head = step // (G // 2)
    turned = query_ref[...].T
    value_span = pl.ds(pl.multiple_of(head * HD, HD), HD)
    finished = []
    for tile in range(rows // WIN):
        span = slice(tile * WIN, (tile + 1) * WIN)
        u = low + (tile - 1) * WIN + lax.broadcasted_iota(jnp.int32, (2 * WIN, WIN), 0)
        t = low + tile * WIN + lax.broadcasted_iota(jnp.int32, (2 * WIN, WIN), 1)
        kept = (u <= t) & (u > t - WIN) & (u >= start_ref[:1, span])
        parts = []
        for e in range(2):
            col = turned[e * HD : (e + 1) * HD, span]
            if heads > 1:
                empty = jnp.zeros_like(col)
                col = jnp.concatenate(
                    [jnp.where(head == i, col, empty) for i in range(heads)], axis=0
                )
            sink = sink_ref[2 * step + e] * LOG2E
            state = (
                jnp.full((1, WIN), sink, jnp.float32),
                jnp.ones((1, WIN), jnp.float32),
                jnp.zeros((HD, WIN), jnp.float32),
            )
            key_span = slice(tile * WIN, (tile + 2) * WIN)
            top, total, acc = fold_in(state, keys[key_span], col, values[value_span, key_span], kept)
            parts.append(acc / total)
        finished.append(jnp.concatenate(parts, axis=0).T.astype(jnp.bfloat16))
    if pieces:
        side = where_ref[2]
        out_refs[0][...] = jnp.where(side == 0, finished[0], finished[1])
        out_refs[1][...] = jnp.where(side == 0, finished[1], finished[0])
    else:
        for tile, value in enumerate(finished):
            out_refs[0][tile * WIN : (tile + 1) * WIN] = value


def band_call(where, starts, sinks, queries, keys, value_rows, rim, heads, rows, pieces, columns):
    steps = heads * G // 2
    width = heads * HD
    smem = pl.BlockSpec(memory_space=pltpu.SMEM)
    if pieces:
        out_shape = [
            jax.ShapeDtypeStruct((WIN, columns), jnp.bfloat16),
            jax.ShapeDtypeStruct((WIN, steps * 128), jnp.bfloat16),
        ]
        out_specs = [
            pl.BlockSpec((WIN, 128), lambda j, w: (0, w[2] * steps + j)),
            pl.BlockSpec((WIN, 128), lambda j, w: (0, j)),
        ]
    else:
        out_shape = [jax.ShapeDtypeStruct((rows, steps * 128), jnp.bfloat16)]
        out_specs = [pl.BlockSpec((rows, 128), lambda j, w: (0, j))]
    fixed = lambda j, w: (0, 0)
    return pl.pallas_call(
        functools.partial(band_body, heads, rows, pieces),
        out_shape=out_shape,
        grid_spec=pltpu.PrefetchScalarGridSpec(
            num_scalar_prefetch=1,
            grid=(steps,),
            in_specs=[
                smem,
                smem,
                pl.BlockSpec((rows, 128), lambda j, w: (0, j)),
                pl.BlockSpec((rows, width), fixed),
                pl.BlockSpec((rows, width), fixed),
                pl.BlockSpec((WIN, 2 * width), fixed),
            ],
            out_specs=out_specs,
            scratch_shapes=[
                pltpu.VMEM((rows + WIN, width), jnp.bfloat16),
                pltpu.VMEM((width, rows + WIN), jnp.bfloat16),
                pltpu.VMEM((8, rows), jnp.int32),
            ],
        ),
        compiler_params=pltpu.CompilerParams(
            dimension_semantics=("arbitrary",), vmem_limit_bytes=48 * 1024 * 1024
        ),
        name="band_attention",
    )(where, starts, sinks, queries, keys, value_rows, rim)


def shifted(value, steps):
    count = lax.axis_size("seq")
    return lax.ppermute(value, "seq", [(i, i + steps) for i in range(count - steps)])


def swapped(value, bit):
    count = lax.axis_size("seq")
    return lax.ppermute(value, "seq", [(i, i ^ bit) for i in range(count)])


def relay(result):
    return lax.all_to_all(result, "kv", split_axis=0, concat_axis=1, tiled=True)


def paired_program(
    q_band, k_band, v_band, sink_band, q_doc, k_doc, v_doc, sink_doc, doc_starts, source_lists
):
    rows = q_band.shape[0]
    heads = k_band.shape[1] // HD
    mine = heads // 2
    width = mine * HD
    columns = 2 * q_band.shape[1]
    shard, side = lax.axis_index("seq"), lax.axis_index("kv")
    core = shard % 2
    layer = shard // 2 % 2
    flip = 4 * layer - 2

    def place(*dists):
        return jnp.stack([shard, core, side, 2 * side + core, *dists]).astype(jnp.int32)

    listed = jnp.zeros((16, 2 * width), jnp.bfloat16)
    listed = lax.dynamic_update_slice(listed, source_lists.astype(jnp.bfloat16), (0, 0))

    def half(value, which, size):
        return lax.dynamic_slice_in_dim(value, which * size, size, axis=1)

    away = jnp.concatenate([half(k_doc, 1 - core, width), half(v_doc, 1 - core, width)], axis=1)
    away = jnp.concatenate([away, listed], axis=0)
    near = swapped(away, 1)
    kept = jnp.concatenate([half(k_doc, core, width), half(v_doc, core, width)], axis=1)
    unit = jnp.concatenate([kept, near[:rows]], axis=0)
    rim = jnp.concatenate([k_band[rows - WIN :], v_band[rows - WIN :]], axis=1)
    rim = shifted(rim, 1)
    q_mate = swapped(half(q_doc, 1 - core, mine * G * HD), 1)
    back4 = shifted(unit, 4)
    back8 = shifted(unit, 8)
    cross0 = swapped(unit, 2)
    cross4 = swapped(back4, 2)
    cross8 = swapped(back8, 2)
    band_out, band_send = band_call(
        place(), doc_starts, sink_band, q_band, k_band, v_band, rim, heads, rows, True, columns
    )
    band_got = lax.ppermute(band_send, "kv", [(0, 1), (1, 0)])
    out_band = lax.dynamic_update_slice(band_out, band_got, (0, (1 - side) * q_band.shape[1]))

    def doc(first, last, units, dists, state):
        plan = DocPlan(first, last, 2, mine, len(units), rows, True)
        return doc_call(
            plan, place(*dists), doc_starts, source_lists, sink_doc, near, (q_doc, q_mate), units, state, columns
        )

    state = doc(True, False, (unit, cross0), (0, flip), None)
    state = doc(False, False, (back4, cross4), (4, 4 + flip), state)
    out_doc, *sends = doc(False, True, (back8, cross8), (8, 8 + flip), state)
    size = mine * G * HD
    for mask, send in zip((1, 2, 3), sends):
        count = 2 * lax.axis_size("seq")
        got = lax.ppermute(send, ("seq", "kv"), [(i, i ^ mask) for i in range(count)])
        source = ((2 * side + core) ^ (mask & 1) * 2 ^ (mask >> 1)) * size
        out_doc = lax.dynamic_update_slice(out_doc, got, (0, source))
    return out_band, out_doc


def plain_program(
    q_band, k_band, v_band, sink_band, q_doc, k_doc, v_doc, sink_doc, doc_starts, source_lists
):
    rows = q_band.shape[0]
    heads = k_band.shape[1] // HD
    shard = lax.axis_index("seq")

    def place(*dists):
        return jnp.stack([shard, 0, 0, 0, *dists]).astype(jnp.int32)

    rim = jnp.concatenate([k_band[rows - WIN :], v_band[rows - WIN :]], axis=1)
    rim = shifted(rim, 1)
    unit = jnp.concatenate([k_doc, v_doc], axis=1)
    units = [unit] + [shifted(unit, d) for d in range(1, BACK + 1)]
    band = band_call(
        place(), doc_starts, sink_band, q_band, k_band, v_band, rim, heads, rows, False, None
    )[0]
    plan = DocPlan(True, True, 1, heads, BACK + 1, rows, False)
    doc = doc_call(
        plan, place(*range(BACK + 1)), doc_starts, source_lists, sink_doc, None,
        (q_doc,), units, None, None,
    )[0]
    return relay(band), relay(doc)


def solution(mesh):
    placed = (
        P("seq", "kv"),
        P("seq", "kv"),
        P("seq", "kv"),
        P("kv"),
        P("seq", "kv"),
        P("seq", "kv"),
        P("seq", "kv"),
        P("kv"),
        P(),
        P("seq", None),
    )

    def per_device(*args):
        heads = args[1].shape[1] // HD
        even = heads % 4 == 0 and mesh.shape["kv"] == 2 and mesh.shape["seq"] % 4 == 0
        return (paired_program if even else plain_program)(*args)

    return jax.shard_map(
        per_device,
        mesh=mesh,
        in_specs=placed,
        out_specs=(P(("seq", "kv"), None), P(("seq", "kv"), None)),
        check_vma=False,
    )
```

profile of v0, /device:TPU:27, one launch (start us, length us, event | category | flops | bytes accessed | tf_op | source)
XLA Modules:
  0.0 165.7 jit_solution(2595770081480746807)
XLA Ops:
  0.7 0.8 convert_element_type.3
  1.5 1.6 constant_dynamic-slice_fusion
  3.1 0.7 collective-permute-start.2
  3.9 1.9 %constant_dynamic-slice_fusion.2 = bf16[256,1024]{1,0:T(8,128)(2,1)} fusion(bf16[256,2048]{1,0:T(8,128)(2,1)} %refs_5_.5, s32[]{:T(128)S(6)} %select_n.43), kind=kLoop, calls=%fused_computation.10 | loop fusion | bytes 1048580 | tf_op jit(solution)/shard_map/dynamic_slice | solution.py:391
  5.9 0.7 pad_maximum_fusion.1
  6.5 1.3 collective-permute-start
  7.8 0.9 pad_maximum_fusion.refs_7_
  8.7 1.3 collective-permute-start.6
  10.0 1.3 collective-permute-start.4
  12.1 22.7 %band_attention.1 = (bf16[128,4096]{1,0:T(8,128)(2,1)}, bf16[128,2048]{1,0:T(8,128)(2,1)}) custom-call(s32[4]{0:T(128)S(1)} %pad_add_fusion.where_ref, s32[16]{0:T(128)S(1)} %copy-done.4, f32[32]{0:T(128)S(1)} %copy-done.7, bf16[256,2048]{1,0:T(8,128)(2,1)S(1)} %copy-done.1, bf16[256,256]{1,0:T(8,128)(2,1)S(1)} %copy-done.2, bf16[256,256]{1,0:T(8,128)(2,1)S(1)} %copy-done.3, ...), custom_call_target="tpu_custom_call" | custom-call | tf_op jit(solution)/shard_map/band_attention/pallas_call | solution.py:329
  34.8 1.2 collective-permute-start.1
  36.0 2.4 %collective-permute-start.8 = (bf16[512,256]{1,0:T(8,128)(2,1)S(1)}, bf16[512,256]{1,0:T(8,128)(2,1)S(1)}, u32[]{:S(2)}, u32[]{:S(2)}) collective-permute-start(bf16[512,256]{1,0:T(8,128)(2,1)S(1)} %pad_maximum_fusion.refs_7_), channel_id=1, source_target_pairs={{0,4},{2,6},{4,0},{6,2},{8,12},{10,14},{12,8},{14,10},{16,20},{18,... | collective-permute-start | bytes 786440 | tf_op jit(solution)/shard_map/ppermute | solution.py:364
  38.5 1.4 collective-permute-start.5
  40.1 3.3 %collective-permute-done.8.refs_8_ = bf16[512,256]{1,0:T(8,128)(2,1)S(1)} collective-permute-done((bf16[512,256]{1,0:T(8,128)(2,1)S(1)}, bf16[512,256]{1,0:T(8,128)(2,1)S(1)}, u32[]{:S(2)}, u32[]{:S(2)}) %collective-permute-start.8) | collective-permute-done | bytes 262176 | tf_op jit(solution)/shard_map/ppermute | solution.py:364
  44.1 41.1 %doc_attention.3 = (f32[8,128,512]{2,1,0:T(8,128)S(1)}, f32[8,8,512]{2,1,0:T(8,128)S(1)}) custom-call(s32[6]{0:T(128)S(1)} %stack.55.refs_0_, s32[16]{0:T(128)S(1)} %copy-done.4, s32[1,8]{1,0:T(1,128)S(1)} %copy-done.5, f32[32]{0:T(128)S(1)} %copy-done.6, bf16[272,256]{1,0:T(8,128)(2,1)S(1)} %collective-permute-done.2.refs_4_, ...), custom_call_target="tpu_custom_call" | custom-call | tf_op jit(solution)/shard_map/doc_attention/pallas_call | solution.py:233
  85.2 47.1 %doc_attention.4 = (f32[8,128,512]{2,1,0:T(8,128)S(1)}, f32[8,8,512]{2,1,0:T(8,128)S(1)}) custom-call(s32[6]{0:T(128)S(1)} %stack.53.refs_0_, s32[16]{0:T(128)S(1)} %copy-done.4, s32[1,8]{1,0:T(1,128)S(1)} %copy-done.5, f32[32]{0:T(128)S(1)} %copy-done.6, ...), custom_call_target="tpu_custom_call", output_to_operand_aliasing={{0}: (9, {}), {1}: (10, {})} | custom-call | tf_op jit(solution)/shard_map/doc_attention/pallas_call | solution.py:233
  132.3 17.2 %doc_attention.5 = (bf16[128,4096]{1,0:T(8,128)(2,1)}, bf16[128,1024]{1,0:T(8,128)(2,1)S(1)}, bf16[128,1024]{1,0:T(8,128)(2,1)S(1)}, bf16[128,1024]{1,0:T(8,128)(2,1)S(1)}) custom-call(s32[6]{0:T(128)S(1)} %stack.51.refs_0_, s32[16]{0:T(128)S(1)} %copy-done.4, s32[1,8]{1,0:T(1,128)S(1)} %copy-done.5, f32[32]{0:T(128)S(1)} %copy-done.6, ...), custom_call_target="tpu_custom_call" | custom-call | tf_op jit(solution)/shard_map/doc_attention/pallas_call | solution.py:233
  149.7 4.5 %collective-permute-start.10 = (bf16[128,1024]{1,0:T(8,128)(2,1)S(1)}, bf16[128,1024]{1,0:T(8,128)(2,1)S(1)}, u32[]{:S(2)}, u32[]{:S(2)}) collective-permute-start(bf16[128,1024]{1,0:T(8,128)(2,1)S(1)} %get-tuple-element.20), channel_id=1, source_target_pairs={{0,2},{1,3},{2,0},{3,1},{4,6},{5,7},{6,4},{7,5},{8,10},{9,11},{10,... | collective-permute-start | bytes 786440 | tf_op jit(solution)/shard_map/ppermute | solution.py:424
  154.2 1.1 collective-permute-start.11
  155.4 0.8 constant_dynamic-update-slice_fusion.3
  156.2 0.7 constant_dynamic-update-slice_fusion.2
  156.9 0.7 constant_dynamic-update-slice_fusion.1
  157.7 7.3 %collective-permute-done.11 = bf16[128,1024]{1,0:T(8,128)(2,1)S(1)} collective-permute-done((bf16[128,1024]{1,0:T(8,128)(2,1)S(1)}, bf16[128,1024]{1,0:T(8,128)(2,1)S(1)}, u32[]{:S(2)}, u32[]{:S(2)}) %collective-permute-start.11) | collective-permute-done | bytes 262176 | tf_op jit(solution)/shard_map/ppermute | solution.py:424
  165.0 0.7 constant_dynamic-update-slice_fusion
  (39 shorter events, 2.1 us)
Async XLA Ops:
  0.6 5.2 %slice-start.1 = ((bf16[256,256]{1,0:T(8,128)(2,1)}), bf16[128,256]{1,0:T(8,128)(2,1)S(1)}, s32[]{:S(2)}) async-start(bf16[256,256]{1,0:T(8,128)(2,1)} %value_ref.1), calls=%async_computation.1 | async-start | bytes 131072 | tf_op jit(solution)/shard_map/slice | solution.py:398
  0.6 10.8 %copy-start.3 = (bf16[256,256]{1,0:T(8,128)(2,1)S(1)}, bf16[256,256]{1,0:T(8,128)(2,1)}, u32[]{:S(2)}) copy-start(bf16[256,256]{1,0:T(8,128)(2,1)} %value_ref.1) | copy-start | bytes 393220
  0.7 5.2 %slice-start = ((bf16[256,256]{1,0:T(8,128)(2,1)}), bf16[128,256]{1,0:T(8,128)(2,1)S(1)}, s32[]{:S(2)}) async-start(bf16[256,256]{1,0:T(8,128)(2,1)} %key_ref.1), calls=%async_computation | async-start | bytes 131072 | tf_op jit(solution)/shard_map/slice | solution.py:398
  0.7 10.8 %copy-start.2 = (bf16[256,256]{1,0:T(8,128)(2,1)S(1)}, bf16[256,256]{1,0:T(8,128)(2,1)}, u32[]{:S(2)}) copy-start(bf16[256,256]{1,0:T(8,128)(2,1)} %key_ref.1) | copy-start | bytes 393220
  0.7 10.8 %copy-start.4 = (s32[16]{0:T(128)S(1)}, s32[16]{0:T(128)}, u32[]{:S(2)}) copy-start(s32[16]{0:T(128)} %refs_1_.5) | copy-start | bytes 196
  0.7 10.8 %copy-start.1 = (bf16[256,2048]{1,0:T(8,128)(2,1)S(1)}, bf16[256,2048]{1,0:T(8,128)(2,1)}, u32[]{:S(2)}) copy-start(bf16[256,2048]{1,0:T(8,128)(2,1)} %query_ref.1) | copy-start | bytes 3145732
  3.1 40.3 %copy-start = (bf16[256,2048]{1,0:T(8,128)(2,1)S(1)}, bf16[256,2048]{1,0:T(8,128)(2,1)}, u32[]{:S(2)}) copy-start(bf16[256,2048]{1,0:T(8,128)(2,1)} %refs_5_.5) | copy-start | bytes 3145732
  3.1 40.3 %copy-start.5 = (s32[1,8]{1,0:T(1,128)S(1)}, s32[1,8]{1,0:T(1,128)}, u32[]{:S(2)}) copy-start(s32[1,8]{1,0:T(1,128)} %refs_2_.5) | copy-start | bytes 100
  3.1 4.7 %collective-permute-start.2 = (bf16[272,256]{1,0:T(8,128)(2,1)S(1)}, bf16[272,256]{1,0:T(8,128)(2,1)S(1)}, u32[]{:S(2)}, u32[]{:S(2)}) collective-permute-start(bf16[272,256]{1,0:T(8,128)(2,1)S(1)} %fusion.1), channel_id=1, source_target_pairs={{0,2},{2,0},{4,6},{6,4},{8,10},{10,8},{12,14},{14,12},{16,18},{18,... | collective-permute-start | bytes 417800 | tf_op jit(solution)/shard_map/ppermute | solution.py:364
  5.8 37.7 %collective-permute-start.3 = (bf16[256,1024]{1,0:T(8,128)(2,1)}, bf16[256,1024]{1,0:T(8,128)(2,1)S(1)}, u32[]{:S(2)}, u32[]{:S(2)}) collective-permute-start(bf16[256,1024]{1,0:T(8,128)(2,1)} %constant_dynamic-slice_fusion.2), channel_id=1, source_target_pairs={{0,2},{2,0},{4,6},{6,4},{8,10},{10,8},{12,14},{14,12},{16,18},{18,... | collective-permute-start | bytes 1572872 | tf_op jit(solution)/shard_map/ppermute | solution.py:364
  6.5 4.9 %collective-permute-start = (bf16[128,512]{1,0:T(8,128)(2,1)}, bf16[128,512]{1,0:T(8,128)(2,1)S(1)}, u32[]{:S(2)}, u32[]{:S(2)}) collective-permute-start(bf16[128,512]{1,0:T(8,128)(2,1)} %pad_maximum_fusion.1), channel_id=1, source_target_pairs={{0,2},{2,4},{4,6},{6,8},{8,10},{10,12},{12,14},{14,16},{16,18},{18... | collective-permute-start | bytes 393224 | tf_op jit(solution)/shard_map/ppermute | solution.py:359
  8.7 29.7 %collective-permute-start.6 = (bf16[512,256]{1,0:T(8,128)(2,1)S(1)}, bf16[512,256]{1,0:T(8,128)(2,1)}, u32[]{:S(2)}, u32[]{:S(2)}) collective-permute-start(bf16[512,256]{1,0:T(8,128)(2,1)S(1)} %pad_maximum_fusion.refs_7_), channel_id=1, source_target_pairs={{0,8},{2,10},{4,12},{6,14},{8,16},{10,18},{12,20},{14,22},{16,24},... | collective-permute-start | bytes 786440 | tf_op jit(solution)/shard_map/ppermute | solution.py:359
  10.0 28.4 %collective-permute-start.4 = (bf16[512,256]{1,0:T(8,128)(2,1)S(1)}, bf16[512,256]{1,0:T(8,128)(2,1)}, u32[]{:S(2)}, u32[]{:S(2)}) collective-permute-start(bf16[512,256]{1,0:T(8,128)(2,1)S(1)} %pad_maximum_fusion.refs_7_), channel_id=1, source_target_pairs={{0,16},{2,18},{4,20},{6,22},{8,24},{10,26},{12,28},{14,30},{1,17},... | collective-permute-start | bytes 786440 | tf_op jit(solution)/shard_map/ppermute | solution.py:359
  11.5 0.7 copy-start.7
  34.8 120.6 %collective-permute-start.1 = (bf16[128,2048]{1,0:T(8,128)(2,1)}, bf16[128,2048]{1,0:T(8,128)(2,1)S(1)}, u32[]{:S(2)}, u32[]{:S(2)}) collective-permute-start(bf16[128,2048]{1,0:T(8,128)(2,1)} %get-tuple-element.13), channel_id=1, source_target_pairs={{0,1},{1,0},{2,3},{3,2},{4,5},{5,4},{6,7},{7,6},{8,9},{9,8},{10,11... | collective-permute-start | bytes 1572872 | tf_op jit(solution)/shard_map/ppermute | solution.py:409
  36.0 7.4 %collective-permute-start.8 = (bf16[512,256]{1,0:T(8,128)(2,1)S(1)}, bf16[512,256]{1,0:T(8,128)(2,1)S(1)}, u32[]{:S(2)}, u32[]{:S(2)}) collective-permute-start(bf16[512,256]{1,0:T(8,128)(2,1)S(1)} %pad_maximum_fusion.refs_7_), channel_id=1, source_target_pairs={{0,4},{2,6},{4,0},{6,2},{8,12},{10,14},{12,8},{14,10},{16,20},{18,... | collective-permute-start | bytes 786440 | tf_op jit(solution)/shard_map/ppermute | solution.py:364
  38.4 46.7 %collective-permute-start.7 = (bf16[512,256]{1,0:T(8,128)(2,1)}, bf16[512,256]{1,0:T(8,128)(2,1)S(1)}, u32[]{:S(2)}, u32[]{:S(2)}) collective-permute-start(bf16[512,256]{1,0:T(8,128)(2,1)} %collective-permute-done.6.refs_7_), channel_id=1, source_target_pairs={{0,4},{2,6},{4,0},{6,2},{8,12},{10,14},{12,8},{14,10},{16,20},{18,... | collective-permute-start | bytes 786440 | tf_op jit(solution)/shard_map/ppermute | solution.py:364
  38.5 93.9 %collective-permute-start.5 = (bf16[512,256]{1,0:T(8,128)(2,1)}, bf16[512,256]{1,0:T(8,128)(2,1)S(1)}, u32[]{:S(2)}, u32[]{:S(2)}) collective-permute-start(bf16[512,256]{1,0:T(8,128)(2,1)} %collective-permute-done.4.refs_7_), channel_id=1, source_target_pairs={{0,4},{2,6},{4,0},{6,2},{8,12},{10,14},{12,8},{14,10},{16,20},{18,... | collective-permute-start | bytes 786440 | tf_op jit(solution)/shard_map/ppermute | solution.py:364
  43.4 0.7 copy-start.6
  149.5 6.7 %collective-permute-start.9 = (bf16[128,1024]{1,0:T(8,128)(2,1)S(1)}, bf16[128,1024]{1,0:T(8,128)(2,1)S(1)}, u32[]{:S(2)}, u32[]{:S(2)}) collective-permute-start(bf16[128,1024]{1,0:T(8,128)(2,1)S(1)} %get-tuple-element.19), channel_id=1, source_target_pairs={{0,1},{1,0},{2,3},{3,2},{4,5},{5,4},{6,7},{7,6},{8,9},{9,8},{10,11... | collective-permute-start | bytes 786440 | tf_op jit(solution)/shard_map/ppermute | solution.py:424
  149.7 7.2 %collective-permute-start.10 = (bf16[128,1024]{1,0:T(8,128)(2,1)S(1)}, bf16[128,1024]{1,0:T(8,128)(2,1)S(1)}, u32[]{:S(2)}, u32[]{:S(2)}) collective-permute-start(bf16[128,1024]{1,0:T(8,128)(2,1)S(1)} %get-tuple-element.20), channel_id=1, source_target_pairs={{0,2},{1,3},{2,0},{3,1},{4,6},{5,7},{6,4},{7,5},{8,10},{9,11},{10,... | collective-permute-start | bytes 786440 | tf_op jit(solution)/shard_map/ppermute | solution.py:424
  154.2 10.7 %collective-permute-start.11 = (bf16[128,1024]{1,0:T(8,128)(2,1)S(1)}, bf16[128,1024]{1,0:T(8,128)(2,1)S(1)}, u32[]{:S(2)}, u32[]{:S(2)}) collective-permute-start(bf16[128,1024]{1,0:T(8,128)(2,1)S(1)} %get-tuple-element.21), channel_id=1, source_target_pairs={{0,3},{1,2},{2,1},{3,0},{4,7},{5,6},{6,5},{7,4},{8,11},{9,10},{10,... | collective-permute-start | bytes 786440 | tf_op jit(solution)/shard_map/ppermute | solution.py:424
where the time goes:
time: 166 us
  Pallas kernels  128 us (77%)
  starting transfers between devices  15.7 us (9%)
  waiting for transfers between devices  10.6 us (6%)
  local copies, waits for them, and re-layouts  8.08 us (5%)
  other arithmetic  2.45 us (1%)
    pallas_call x3, Pallas kernels, doc_call(): pl.pallas_call(functools.partial(doc_body, plan), out_shape=out_shape, gr...  105 us
    pallas_call x1, Pallas kernels, band_call(): pl.pallas_call(functools.partial(band_body, heads, rows, pieces), out_sha...  22.7 us
    ppermute x3, waiting for transfers between devices, paired_program(): lax.ppermute(send, ('seq', 'kv'), [(i, i ^ mask) for i in range(count)])  7.32 us
    ppermute x3, starting transfers between devices, paired_program(): lax.ppermute(send, ('seq', 'kv'), [(i, i ^ mask) for i in range(count)])  5.88 us
    ppermute x5, starting transfers between devices, swapped(): return lax.ppermute(value, 'seq', [(i, i ^ bit) for i in range(count)])  4.68 us
    ppermute x3, starting transfers between devices, shifted(): lax.ppermute(value, 'seq', [(i, i + steps) for i in range(count - steps)])  3.86 us
    dynamic_slice x2, local copies, waits for them, and re-layouts, half(): return lax.dynamic_slice_in_dim(value, which * size, size, axis=1)  3.48 us
  transfers between devices with their start and end apart: 12, of which 2 were waited for; matrix products, arithmetic and copies ran while one was open for 4% of the time, Pallas kernels for 77%

commit v1 on v0

v1 whole, which is shorter than its diff:
```python
import functools
import jax
import jax.numpy as jnp
from jax import lax
from jax.experimental import pallas as pl
from jax.experimental.pallas import tpu as pltpu
from jax.sharding import PartitionSpec as P

HD = 64
G = 8
WIN = 128
BACK = 8
LOG2E = 1.4426950408889634
SCORE_SCALE = HD ** (-0.5) * LOG2E
NEG = -1e30
SAFE_TOTAL = 2.0**100
NEVER = 2**30
PARAMS = pltpu.CompilerParams(
    dimension_semantics=("arbitrary",), vmem_limit_bytes=48 * 1024 * 1024
)


def start_of(starts_ref, position):
    found = jnp.int32(0)
    for i in range(starts_ref.shape[0]):
        entry = starts_ref[i]
        found = jnp.where(entry <= position, jnp.maximum(found, entry), found)
    return found


def start_row(starts_ref, positions):
    found = jnp.zeros_like(positions)
    for i in range(starts_ref.shape[0]):
        entry = starts_ref[i]
        found = jnp.where(positions >= entry, jnp.maximum(found, entry), found)
    return found


def score(key_block, query_cols):
    return jnp.dot(key_block, query_cols, preferred_element_type=jnp.float32) * SCORE_SCALE


def plain_weights(key_block, query_cols, kept):
    weight = jnp.where(kept, jnp.exp2(score(key_block, query_cols)), 0.0)
    return weight.astype(jnp.bfloat16), jnp.sum(weight, axis=0, keepdims=True)


def weigh(value_rows, weight):
    return jnp.dot(value_rows, weight, preferred_element_type=jnp.float32)


def topped(state, key_block, query_cols, value_rows, kept):
    top, total, acc = state
    scores = jnp.where(kept, score(key_block, query_cols), NEG)
    new_top = jnp.maximum(top, jnp.max(scores, axis=0, keepdims=True))
    weight = jnp.exp2(scores - new_top)
    fading = jnp.exp2(top - new_top)
    total = total * fading + jnp.sum(weight, axis=0, keepdims=True)
    acc = acc * fading + weigh(value_rows, weight.astype(jnp.bfloat16))
    return new_top, total, acc


def slotted(col, head, heads):
    if heads == 1:
        return col
    empty = jnp.zeros_like(col)
    return jnp.concatenate([jnp.where(head == i, col, empty) for i in range(heads)], axis=0)


def overflowed(total):
    return jnp.logical_not(jnp.max(total) <= SAFE_TOTAL)


def sink_lanes(sink_ref, first, count, rows):
    return jnp.concatenate(
        [jnp.full((1, rows), sink_ref[first + e] * LOG2E, jnp.float32) for e in range(count)], axis=1
    )


class DocPlan:
    def __init__(self, first, last, grp, heads, earlier, units, rows, pieces):
        self.first, self.last, self.grp, self.heads = first, last, grp, heads
        self.earlier, self.units, self.rows, self.pieces = earlier, units, rows, pieces


def doc_body(plan, *refs):
    first, last, grp, heads, rows = plan.first, plan.last, plan.grp, plan.heads, plan.rows
    count = plan.earlier + plan.units
    refs = list(refs)
    where_ref, starts_ref, list_ref, sink_ref = refs[:4]
    del refs[:4]
    mate_list_ref = refs.pop(0) if grp == 2 else None
    query_refs = [refs.pop(0) for _ in range(grp)]
    unit_refs = [refs.pop(0) for _ in range(count)]
    if not first:
        acc_in, total_in = refs.pop(0), refs.pop(0)
    if last:
        piece_refs = [refs.pop(0) for _ in range(2 * grp if plan.pieces else 1)]
    else:
        acc_out, total_out = refs.pop(0), refs.pop(0)
    value_ref, bound_ref, flag_ref, acc_ref, total_ref = refs
    step = pl.program_id(0)
    own_shard = where_ref[0]
    shards = [own_shard, own_shard ^ 1][:grp]
    width = heads * HD
    lanes = 2 * grp * rows
    new = range(plan.earlier, count)

    def key_shard(n, r):
        return shards[r] - where_ref[4 + n]

    @pl.when(step == 0)
    def _():
        for n in range(count):
            unit = unit_refs[n][...]
            value_ref[n] = unit[:, width:].T if width % 128 == 0 else unit.T[width:]
        for n in range(count):
            flag_ref[n] = 0
        for a in range(grp):
            q_low = shards[a] * rows
            start_low = start_of(starts_ref, q_low)
            positions = q_low + lax.broadcasted_iota(jnp.int32, (1, rows), 1)
            starts = start_row(starts_ref, positions)
            if a == 1:
                mate_row = mate_list_ref[...].astype(jnp.float32)[:1]
                listed = lax.broadcasted_iota(jnp.int32, mate_row.shape, 1) < BACK
            for n in range(count):
                for r in range(grp):
                    shard = key_shard(n, r)
                    named = shard == shards[a]
                    if a == 0:
                        for i in range(BACK):
                            named = named | (list_ref[0, i] == shard)
                    else:
                        same = (mate_row == shard.astype(jnp.float32)) & listed
                        named = named | (jnp.max(same.astype(jnp.float32)) > 0.5)
                    named = named & (shard >= 0) & (shard <= shards[a])
                    live = named & ((shard + 1) * rows > start_low)
                    flag_ref[n] = flag_ref[n] | live.astype(jnp.int32)
                    bound = jnp.where(named, starts, NEVER)
                    spot = slice(2 * a * rows, 2 * (a + 1) * rows)
                    bound_ref[n, r : r + 1, spot] = jnp.concatenate([bound, bound], axis=1)

    head = step // (G // 2)
    sinks = sink_lanes(sink_ref, where_ref[1] * heads * G + 2 * step, 2, rows)
    sinks = jnp.concatenate([sinks] * grp, axis=1)
    if first:
        total_ref[...] = jnp.exp2(sinks)
        acc_ref[...] = jnp.zeros((HD, lanes), jnp.float32)
    else:
        total_ref[...] = total_in[0]
        acc_ref[...] = acc_in[0]
    cols = []
    for a in range(grp):
        turned = query_refs[a][...].T
        cols += [slotted(turned[e * HD : (e + 1) * HD], head, heads) for e in range(2)]
    cols = jnp.concatenate(cols, axis=1)
    value_span = pl.ds(pl.multiple_of(head * HD, HD), HD)

    def keep(n, r):
        u = key_shard(n, r) * rows + lax.broadcasted_iota(jnp.int32, (rows, lanes), 0)
        kept = u >= bound_ref[n, r : r + 1]
        if n == 0:
            lane = lax.broadcasted_iota(jnp.int32, (1, lanes), 1)
            t = jnp.bitwise_and(lane, rows - 1) + own_shard * rows
            if grp == 2:
                t = jnp.where(lane < 2 * rows, t, t + ((own_shard ^ 1) - own_shard) * rows)
            kept = kept & (u <= t)
        return kept

    def keys_of(n, r):
        return unit_refs[n][r * rows : (r + 1) * rows, :width]

    def values_of(n, r=None):
        span = slice(None) if r is None else slice(r * rows, (r + 1) * rows)
        return value_ref[n, value_span, span]

    def work(n):
        total = total_ref[...]
        weights = []
        for r in range(grp):
            weight, part = plain_weights(keys_of(n, r), cols, keep(n, r))
            weights.append(weight)
            total = total + part
        total_ref[...] = total
        acc_ref[...] += weigh(values_of(n), jnp.concatenate(weights, axis=0))

    for n in new:
        pl.when(flag_ref[n] > 0)(functools.partial(work, n))

    if not last:
        acc_out[0] = acc_ref[...]
        total_out[0] = total_ref[...]
        return

    @pl.when(overflowed(total_ref[...]))
    def _():
        state = sinks, jnp.ones((1, lanes), jnp.float32), jnp.zeros((HD, lanes), jnp.float32)
        for n in range(count):
            for r in range(grp):
                state = topped(state, keys_of(n, r), cols, values_of(n, r), keep(n, r))
        total_ref[...] = state[1]
        acc_ref[...] = state[2]

    result = acc_ref[...] / total_ref[...]
    for a in range(grp):
        parts = [result[:, (2 * a + e) * rows : (2 * a + e + 1) * rows] for e in range(2)]
        block = jnp.concatenate(parts, axis=0).T.astype(jnp.bfloat16)
        if not plan.pieces:
            piece_refs[0][...] = block
            continue
        half = rows // 2
        side = where_ref[2]
        low, high = block[:half], block[half:]
        piece_refs[2 * a][...] = jnp.where(side == 0, low, high)
        piece_refs[2 * a + 1][...] = jnp.where(side == 0, high, low)


def doc_call(plan, where, starts, sources, sinks, mate_rows, queries, units, state, columns):
    grp, heads, rows = plan.grp, plan.heads, plan.rows
    steps = heads * G // 2
    width = heads * HD
    count = plan.earlier + plan.units
    smem = pl.BlockSpec(memory_space=pltpu.SMEM)
    args = [where, starts, sources, sinks]
    specs = [smem, smem, smem]
    if grp == 2:
        args.append(mate_rows)
        specs.append(pl.BlockSpec((16, 128), lambda j, w: (rows // 16, 0)))
    args += list(queries)
    specs.append(pl.BlockSpec((rows, 128), lambda j, w: (0, w[1] * steps + j)))
    if grp == 2:
        specs.append(pl.BlockSpec((rows, 128), lambda j, w: (0, j)))
    for unit in units:
        args.append(unit)
        specs.append(pl.BlockSpec((grp * rows, 2 * width), lambda j, w: (0, 0)))
    lanes = 2 * grp * rows
    state_specs = [
        pl.BlockSpec((1, HD, lanes), lambda j, w: (j, 0, 0)),
        pl.BlockSpec((1, 1, lanes), lambda j, w: (j, 0, 0)),
    ]
    state_shapes = [
        jax.ShapeDtypeStruct((steps, HD, lanes), jnp.float32),
        jax.ShapeDtypeStruct((steps, 1, lanes), jnp.float32),
    ]
    aliases = {}
    if not plan.first:
        if not plan.last:
            aliases = {len(args): 0, len(args) + 1: 1}
        args += list(state)
        specs += state_specs
    if not plan.last:
        out_shape, out_specs = state_shapes, state_specs
    elif plan.pieces:
        half = rows // 2
        out_shape = [jax.ShapeDtypeStruct((half, columns), jnp.bfloat16)]
        out_specs = [pl.BlockSpec((half, 128), lambda j, w: (0, w[3] * steps + j))]
        for _ in range(2 * grp - 1):
            out_shape.append(jax.ShapeDtypeStruct((half, steps * 128), jnp.bfloat16))
            out_specs.append(pl.BlockSpec((half, 128), lambda j, w: (0, j)))
    else:
        out_shape = [jax.ShapeDtypeStruct((rows, steps * 128), jnp.bfloat16)]
        out_specs = [pl.BlockSpec((rows, 128), lambda j, w: (0, j))]
    return pl.pallas_call(
        functools.partial(doc_body, plan),
        out_shape=out_shape,
        grid_spec=pltpu.PrefetchScalarGridSpec(
            num_scalar_prefetch=1,
            grid=(steps,),
            in_specs=specs,
            out_specs=out_specs,
            scratch_shapes=[
                pltpu.VMEM((count, width, grp * rows), jnp.bfloat16),
                pltpu.VMEM((count, grp, lanes), jnp.int32),
                pltpu.SMEM((count,), jnp.int32),
                pltpu.VMEM((HD, lanes), jnp.float32),
                pltpu.VMEM((1, lanes), jnp.float32),
            ],
        ),
        input_output_aliases=aliases,
        compiler_params=PARAMS,
        name="doc_attention",
    )(*args)


def band_body(heads, rows, wide, pieces, where_ref, starts_ref, sink_ref, query_ref, key_ref, value_ref, rim_ref, *refs):
    out_refs, (keys, values, bound_ref, acc_ref, total_ref) = refs[:-5], refs[-5:]
    step = pl.program_id(0)
    width = heads * HD
    low = where_ref[0] * rows
    tiles = rows // WIN
    lanes = wide * WIN

    @pl.when(step == 0)
    def _():
        rim = rim_ref[...]
        keys[:WIN] = rim[:, :width]
        keys[WIN:] = key_ref[...]
        values[:, :WIN] = rim[:, width:].T if width % 128 == 0 else rim.T[width:]
        values[:, WIN:] = value_ref[...].T
        t = low + lax.broadcasted_iota(jnp.int32, (1, rows), 1)
        bound = jnp.maximum(start_row(starts_ref, t), t - (WIN - 1))
        for tile in range(tiles):
            part = bound[:, tile * WIN : (tile + 1) * WIN]
            bound_ref[tile : tile + 1] = jnp.concatenate([part] * wide, axis=1)

    head = step // (G // wide)
    turned = query_ref[...].T
    value_span = pl.ds(pl.multiple_of(head * HD, HD), HD)
    sinks = sink_lanes(sink_ref, wide * step, wide, WIN)

    def cols_of(tile):
        span = slice(tile * WIN, (tile + 1) * WIN)
        cols = [slotted(turned[e * HD : (e + 1) * HD, span], head, heads) for e in range(wide)]
        return jnp.concatenate(cols, axis=1)

    def keep(tile):
        u = lax.broadcasted_iota(jnp.int32, (2 * WIN, lanes), 0) + (low + (tile - 1) * WIN)
        lane = lax.broadcasted_iota(jnp.int32, (1, lanes), 1)
        t = jnp.bitwise_and(lane, WIN - 1) + (low + tile * WIN)
        return (u <= t) & (u >= bound_ref[tile : tile + 1])

    for tile in range(tiles):
        span = slice(tile * WIN, (tile + 2) * WIN)
        weight, part = plain_weights(keys[span], cols_of(tile), keep(tile))
        total_ref[tile : tile + 1] = jnp.exp2(sinks) + part
        acc_ref[tile] = weigh(values[value_span, span], weight)

    @pl.when(overflowed(total_ref[...]))
    def _():
        for tile in range(tiles):
            span = slice(tile * WIN, (tile + 2) * WIN)
            state = sinks, jnp.ones((1, lanes), jnp.float32), jnp.zeros((HD, lanes), jnp.float32)
            state = topped(state, keys[span], cols_of(tile), values[value_span, span], keep(tile))
            total_ref[tile : tile + 1] = state[1]
            acc_ref[tile] = state[2]

    finished = []
    for tile in range(tiles):
        result = acc_ref[tile] / total_ref[tile : tile + 1]
        parts = [result[:, e * WIN : (e + 1) * WIN] for e in range(wide)]
        finished.append(jnp.concatenate(parts, axis=0).T.astype(jnp.bfloat16))
    if pieces:
        side = where_ref[2]
        out_refs[0][...] = jnp.where(side == 0, finished[0], finished[1])
        out_refs[1][...] = jnp.where(side == 0, finished[1], finished[0])
    else:
        for tile, value in enumerate(finished):
            out_refs[0][tile * WIN : (tile + 1) * WIN] = value


def band_call(where, starts, sinks, queries, keys, value_rows, rim, heads, rows, pieces, columns):
    wide = 4
    steps = heads * G // wide
    size = wide * HD
    width = heads * HD
    tiles = rows // WIN
    smem = pl.BlockSpec(memory_space=pltpu.SMEM)
    if pieces:
        out_shape = [
            jax.ShapeDtypeStruct((WIN, columns), jnp.bfloat16),
            jax.ShapeDtypeStruct((WIN, steps * size), jnp.bfloat16),
        ]
        out_specs = [
            pl.BlockSpec((WIN, size), lambda j, w: (0, w[2] * steps + j)),
            pl.BlockSpec((WIN, size), lambda j, w: (0, j)),
        ]
    else:
        out_shape = [jax.ShapeDtypeStruct((rows, steps * size), jnp.bfloat16)]
        out_specs = [pl.BlockSpec((rows, size), lambda j, w: (0, j))]

    def fixed(j, w):
        return (0, 0)

    return pl.pallas_call(
        functools.partial(band_body, heads, rows, wide, pieces),
        out_shape=out_shape,
        grid_spec=pltpu.PrefetchScalarGridSpec(
            num_scalar_prefetch=1,
            grid=(steps,),
            in_specs=[
                smem,
                smem,
                pl.BlockSpec((rows, size), lambda j, w: (0, j)),
                pl.BlockSpec((rows, width), fixed),
                pl.BlockSpec((rows, width), fixed),
                pl.BlockSpec((WIN, 2 * width), fixed),
            ],
            out_specs=out_specs,
            scratch_shapes=[
                pltpu.VMEM((rows + WIN, width), jnp.bfloat16),
                pltpu.VMEM((width, rows + WIN), jnp.bfloat16),
                pltpu.VMEM((tiles, wide * WIN), jnp.int32),
                pltpu.VMEM((tiles, HD, wide * WIN), jnp.float32),
                pltpu.VMEM((tiles, wide * WIN), jnp.float32),
            ],
        ),
        compiler_params=PARAMS,
        name="band_attention",
    )(where, starts, sinks, queries, keys, value_rows, rim)


def shifted(value, steps):
    count = lax.axis_size("seq")
    return lax.ppermute(value, "seq", [(i, i + steps) for i in range(count - steps)])


def swapped(value, bit):
    count = lax.axis_size("seq")
    return lax.ppermute(value, "seq", [(i, i ^ bit) for i in range(count)])


def relay(result):
    return lax.all_to_all(result, "kv", split_axis=0, concat_axis=1, tiled=True)


def paired_program(
    q_band, k_band, v_band, sink_band, q_doc, k_doc, v_doc, sink_doc, doc_starts, source_lists
):
    rows = q_band.shape[0]
    heads = k_band.shape[1] // HD
    mine = heads // 2
    width = mine * HD
    columns = 2 * q_band.shape[1]
    shard, side = lax.axis_index("seq"), lax.axis_index("kv")
    core = shard % 2
    layer = shard // 2 % 2
    flip = 4 * layer - 2

    def place(*dists):
        return jnp.stack([shard, core, side, 2 * side + core, *dists]).astype(jnp.int32)

    listed = jnp.zeros((16, 2 * width), jnp.bfloat16)
    listed = lax.dynamic_update_slice(listed, source_lists.astype(jnp.bfloat16), (0, 0))

    def half(value, which, size):
        return lax.dynamic_slice_in_dim(value, which * size, size, axis=1)

    away = jnp.concatenate([half(k_doc, 1 - core, width), half(v_doc, 1 - core, width)], axis=1)
    away = jnp.concatenate([away, listed], axis=0)
    near = swapped(away, 1)
    kept = jnp.concatenate([half(k_doc, core, width), half(v_doc, core, width)], axis=1)
    unit = jnp.concatenate([kept, near[:rows]], axis=0)
    rim = jnp.concatenate([k_band[rows - WIN :], v_band[rows - WIN :]], axis=1)
    rim = shifted(rim, 1)
    q_mate = swapped(half(q_doc, 1 - core, mine * G * HD), 1)
    back4 = shifted(unit, 4)
    back8 = shifted(unit, 8)
    cross0 = swapped(unit, 2)
    cross4 = swapped(back4, 2)
    cross8 = swapped(back8, 2)
    band_out, band_send = band_call(
        place(), doc_starts, sink_band, q_band, k_band, v_band, rim, heads, rows, True, columns
    )
    band_got = lax.ppermute(band_send, "kv", [(0, 1), (1, 0)])
    out_band = lax.dynamic_update_slice(band_out, band_got, (0, (1 - side) * q_band.shape[1]))

    def doc(first, last, units, dists, earlier, state):
        plan = DocPlan(first, last, 2, mine, earlier, len(units) - earlier, rows, True)
        return doc_call(
            plan, place(*dists), doc_starts, source_lists, sink_doc, near, (q_doc, q_mate), units, state, columns
        )

    units = [unit, cross0, back4, cross4, back8, cross8]
    dists = [0, flip, 4, 4 + flip, 8, 8 + flip]
    state = doc(True, False, units[:3], dists[:3], 0, None)
    state = doc(False, False, units[3:5], dists[3:5], 0, state)
    out_doc, *sends = doc(False, True, units, dists, 5, state)
    size = mine * G * HD
    for mask, send in zip((1, 2, 3), sends):
        count = 2 * lax.axis_size("seq")
        got = lax.ppermute(send, ("seq", "kv"), [(i, i ^ mask) for i in range(count)])
        source = ((2 * side + core) ^ (mask & 1) * 2 ^ (mask >> 1)) * size
        out_doc = lax.dynamic_update_slice(out_doc, got, (0, source))
    return out_band, out_doc


def plain_program(
    q_band, k_band, v_band, sink_band, q_doc, k_doc, v_doc, sink_doc, doc_starts, source_lists
):
    rows = q_band.shape[0]
    heads = k_band.shape[1] // HD
    shard = lax.axis_index("seq")

    def place(*dists):
        return jnp.stack([shard, 0, 0, 0, *dists]).astype(jnp.int32)

    rim = jnp.concatenate([k_band[rows - WIN :], v_band[rows - WIN :]], axis=1)
    rim = shifted(rim, 1)
    unit = jnp.concatenate([k_doc, v_doc], axis=1)
    units = [unit] + [shifted(unit, d) for d in range(1, BACK + 1)]
    band = band_call(
        place(), doc_starts, sink_band, q_band, k_band, v_band, rim, heads, rows, False, None
    )[0]
    plan = DocPlan(True, True, 1, heads, 0, BACK + 1, rows, False)
    doc = doc_call(
        plan, place(*range(BACK + 1)), doc_starts, source_lists, sink_doc, None,
        (q_doc,), units, None, None,
    )[0]
    return relay(band), relay(doc)


def solution(mesh):
    placed = (
        P("seq", "kv"),
        P("seq", "kv"),
        P("seq", "kv"),
        P("kv"),
        P("seq", "kv"),
        P("seq", "kv"),
        P("seq", "kv"),
        P("kv"),
        P(),
        P("seq", None),
    )

    def per_device(*args):
        heads = args[1].shape[1] // HD
        even = heads % 4 == 0 and mesh.shape["kv"] == 2 and mesh.shape["seq"] % 4 == 0
        return (paired_program if even else plain_program)(*args)

    return jax.shard_map(
        per_device,
        mesh=mesh,
        in_specs=placed,
        out_specs=(P(("seq", "kv"), None), P(("seq", "kv"), None)),
        check_vma=False,
    )
```

time: 166 us -> 153 us (0.922)
  Pallas kernels: 128 us -> 112 us
  local copies, waits for them, and re-layouts: 8.08 us -> 11.7 us
  starting transfers between devices: 15.7 us -> 17.4 us
  waiting for transfers between devices: 10.6 us -> 8.94 us
    pallas_call x3, Pallas kernels: 105 us -> 95.6 us  [doc_call(): pl.pallas_call(functools.partial(doc_body, plan), out_shape=out_shape, gr...]
    pallas_call x1, Pallas kernels: 22.7 us -> 16.8 us  [band_call(): pl.pallas_call(functools.partial(band_body, heads, rows, wide, pieces), o...]
    unnamed x16 -> x20, local copies, waits for them, and re-layouts: 1.33 us -> 4.56 us
    ppermute x3, starting transfers between devices: 5.88 us -> 7.58 us  [paired_program(): lax.ppermute(send, ('seq', 'kv'), [(i, i ^ mask) for i in range(count)])]
  transfers between devices with their start and end apart: 12 -> 12, of which waited for: 2 -> 2; matrix products, arithmetic and copies ran while one was open for 4% -> 4% of each run, Pallas kernels for 77% -> 74%
where the time goes in v1:
time: 153 us
  Pallas kernels  112 us (73%)
  starting transfers between devices  17.4 us (11%)
  local copies, waits for them, and re-layouts  11.7 us (8%)
  waiting for transfers between devices  8.94 us (6%)
  other arithmetic  1.54 us (1%)
    pallas_call x3, Pallas kernels, doc_call(): pl.pallas_call(functools.partial(doc_body, plan), out_shape=out_shape, gr...  95.6 us
    pallas_call x1, Pallas kernels, band_call(): pl.pallas_call(functools.partial(band_body, heads, rows, wide, pieces), o...  16.8 us
    ppermute x3, starting transfers between devices, paired_program(): lax.ppermute(send, ('seq', 'kv'), [(i, i ^ mask) for i in range(count)])  7.58 us
    ppermute x3, waiting for transfers between devices, paired_program(): lax.ppermute(send, ('seq', 'kv'), [(i, i ^ mask) for i in range(count)])  6.49 us
    ppermute x5, starting transfers between devices, swapped(): return lax.ppermute(value, 'seq', [(i, i ^ bit) for i in range(count)])  4.68 us
    unnamed x20, local copies, waits for them, and re-layouts  4.56 us
    ppermute x3, starting transfers between devices, shifted(): lax.ppermute(value, 'seq', [(i, i + steps) for i in range(count - steps)])  3.86 us
  transfers between devices with their start and end apart: 12, of which 2 were waited for; matrix products, arithmetic and copies ran while one was open for 4% of the time, Pallas kernels for 74%

profile of v1, /device:TPU:27, one launch (start us, length us, event | category | flops | bytes accessed | tf_op | source)
XLA Modules:
  0.0 152.8 jit_solution(17159084162764416637)
XLA Ops:
  0.7 0.8 convert_element_type.3
  1.5 1.0 constant_dynamic-slice_fusion
  2.5 0.7 collective-permute-start.2
  3.2 1.9 %constant_dynamic-slice_fusion.2 = bf16[256,1024]{1,0:T(8,128)(2,1)} fusion(bf16[256,2048]{1,0:T(8,128)(2,1)} %refs_5_.5, s32[]{:T(128)S(6)} %select_n.43), kind=kLoop, calls=%fused_computation.10 | loop fusion | bytes 1048580 | tf_op jit(solution)/shard_map/dynamic_slice | solution.py:437
  5.8 1.3 collective-permute-start
  7.2 1.3 collective-permute-start.5
  8.5 1.3 collective-permute-start.7
  9.9 0.9 copy-done.2
  10.8 0.9 copy-done.3
  12.4 16.8 %band_attention.1 = (bf16[128,4096]{1,0:T(8,128)(2,1)}, bf16[128,2048]{1,0:T(8,128)(2,1)}) custom-call(s32[4]{0:T(128)S(1)} %pad_add_fusion.where_ref, s32[16]{0:T(128)S(1)} %copy-done.4, f32[32]{0:T(128)S(1)} %copy-done.7, bf16[256,2048]{1,0:T(8,128)(2,1)S(1)} %copy-done.1, bf16[256,256]{1,0:T(8,128)(2,1)S(1)} %copy-done.2, bf16[256,256]{1,0:T(8,128)(2,1)S(1)} %copy-done.3, ...), custom_call_target="tpu_custom_call" | custom-call | tf_op jit(solution)/shard_map/band_attention/pallas_call | solution.py:375
  29.2 1.2 collective-permute-start.1
  30.4 2.4 %collective-permute-start.4 = (bf16[512,256]{1,0:T(8,128)(2,1)S(1)}, bf16[512,256]{1,0:T(8,128)(2,1)S(1)}, u32[]{:S(2)}, u32[]{:S(2)}) collective-permute-start(bf16[512,256]{1,0:T(8,128)(2,1)S(1)} %pad_maximum_fusion.refs_7_), channel_id=1, source_target_pairs={{0,4},{2,6},{4,0},{6,2},{8,12},{10,14},{12,8},{14,10},{16,20},{18,... | collective-permute-start | bytes 786440 | tf_op jit(solution)/shard_map/ppermute | solution.py:410
  32.8 1.4 collective-permute-start.8
  34.5 2.4 %collective-permute-done.4.refs_8_ = bf16[512,256]{1,0:T(8,128)(2,1)S(1)} collective-permute-done((bf16[512,256]{1,0:T(8,128)(2,1)S(1)}, bf16[512,256]{1,0:T(8,128)(2,1)S(1)}, u32[]{:S(2)}, u32[]{:S(2)}) %collective-permute-start.4) | collective-permute-done | bytes 262176 | tf_op jit(solution)/shard_map/ppermute | solution.py:410
  37.6 23.5 %doc_attention.3 = (f32[8,64,1024]{2,1,0:T(8,128)S(1)}, f32[8,1,1024]{2,1,0:T(1,128)S(1)}) custom-call(s32[7]{0:T(128)S(1)} %stack.57.refs_0_, s32[16]{0:T(128)S(1)} %copy-done.4, s32[1,8]{1,0:T(1,128)S(1)} %copy-done.5, f32[32]{0:T(128)S(1)} %copy-done.6, bf16[272,256]{1,0:T(8,128)(2,1)S(1)} %collective-permute-done.2.refs_4_, ...), custom_call_target="tpu_custom_call" | custom-call | tf_op jit(solution)/shard_map/doc_attention/pallas_call | solution.py:264
  61.2 16.9 %doc_attention.4 = (f32[8,64,1024]{2,1,0:T(8,128)S(1)}, f32[8,1,1024]{2,1,0:T(1,128)S(1)}) custom-call(s32[6]{0:T(128)S(1)} %stack.56.refs_0_, s32[16]{0:T(128)S(1)} %copy-done.4, s32[1,8]{1,0:T(1,128)S(1)} %copy-done.5, f32[32]{0:T(128)S(1)} %copy-done.6, ...), custom_call_target="tpu_custom_call", output_to_operand_aliasing={{0}: (9, {}), {1}: (10, {})} | custom-call | tf_op jit(solution)/shard_map/doc_attention/pallas_call | solution.py:264
  78.0 55.2 %doc_attention.5 = (bf16[128,4096]{1,0:T(8,128)(2,1)}, bf16[128,1024]{1,0:T(8,128)(2,1)}, bf16[128,1024]{1,0:T(8,128)(2,1)S(1)}, bf16[128,1024]{1,0:T(8,128)(2,1)S(1)}) custom-call(s32[10]{0:T(128)S(1)} %stack.55.refs_0_, s32[16]{0:T(128)S(1)} %copy-done.4, s32[1,8]{1,0:T(1,128)S(1)} %copy-done.5, f32[32]{0:T(128)S(1)} %copy-done.6, ...), custom_call_target="tpu_custom_call" | custom-call | tf_op jit(solution)/shard_map/doc_attention/pallas_call | solution.py:264
  134.0 0.7 copy-done.9
  134.9 6.2 %collective-permute-start.10 = (bf16[128,1024]{1,0:T(8,128)(2,1)}, bf16[128,1024]{1,0:T(8,128)(2,1)S(1)}, u32[]{:S(2)}, u32[]{:S(2)}) collective-permute-start(bf16[128,1024]{1,0:T(8,128)(2,1)} %copy-done.9), channel_id=1, source_target_pairs={{0,2},{1,3},{2,0},{3,1},{4,6},{5,7},{6,4},{7,5},{8,10},{9,11},{10,... | collective-permute-start | bytes 786440 | tf_op jit(solution)/shard_map/ppermute | solution.py:472
  141.1 1.1 collective-permute-start.11
  142.3 1.9 %constant_dynamic-update-slice_fusion.3 = bf16[128,4096]{1,0:T(8,128)(2,1)} fusion(bf16[128,4096]{1,0:T(8,128)(2,1)} %get-tuple-element.12, bf16[128,2048]{1,0:T(8,128)(2,1)} %collective-permute-done.1, s32[]{:T(128)S(6)} %select_n.39), kind=kLoop, calls=%fused_computation.13 | loop fusion | bytes 1048580 | tf_op jit(solution)/shard_map/dynamic_update_slice | solution.py:456
  144.1 0.7 constant_dynamic-update-slice_fusion.2
  144.9 0.7 constant_dynamic-update-slice_fusion.1
  145.6 6.5 %collective-permute-done.11 = bf16[128,1024]{1,0:T(8,128)(2,1)S(1)} collective-permute-done((bf16[128,1024]{1,0:T(8,128)(2,1)}, bf16[128,1024]{1,0:T(8,128)(2,1)S(1)}, u32[]{:S(2)}, u32[]{:S(2)}) %collective-permute-start.11) | collective-permute-done | bytes 262176 | tf_op jit(solution)/shard_map/ppermute | solution.py:472
  (43 shorter events, 4.2 us)
Async XLA Ops:
  0.6 4.5 %slice-start.1 = ((bf16[256,256]{1,0:T(8,128)(2,1)}), bf16[128,256]{1,0:T(8,128)(2,1)S(1)}, s32[]{:S(2)}) async-start(bf16[256,256]{1,0:T(8,128)(2,1)} %value_ref.1), calls=%async_computation.1 | async-start | bytes 131072 | tf_op jit(solution)/shard_map/slice | solution.py:444
  0.6 4.5 %slice-start = ((bf16[256,256]{1,0:T(8,128)(2,1)}), bf16[128,256]{1,0:T(8,128)(2,1)S(1)}, s32[]{:S(2)}) async-start(bf16[256,256]{1,0:T(8,128)(2,1)} %key_ref.1), calls=%async_computation | async-start | bytes 131072 | tf_op jit(solution)/shard_map/slice | solution.py:444
  0.7 9.2 %copy-start.4 = (s32[16]{0:T(128)S(1)}, s32[16]{0:T(128)}, u32[]{:S(2)}) copy-start(s32[16]{0:T(128)} %refs_1_.5) | copy-start | bytes 196
  0.7 9.2 %copy-start.1 = (bf16[256,2048]{1,0:T(8,128)(2,1)S(1)}, bf16[256,2048]{1,0:T(8,128)(2,1)}, u32[]{:S(2)}) copy-start(bf16[256,2048]{1,0:T(8,128)(2,1)} %query_ref.1) | copy-start | bytes 3145732
  2.4 34.6 %copy-start = (bf16[256,2048]{1,0:T(8,128)(2,1)S(1)}, bf16[256,2048]{1,0:T(8,128)(2,1)}, u32[]{:S(2)}) copy-start(bf16[256,2048]{1,0:T(8,128)(2,1)} %refs_5_.5) | copy-start | bytes 3145732
  2.4 34.5 %copy-start.5 = (s32[1,8]{1,0:T(1,128)S(1)}, s32[1,8]{1,0:T(1,128)}, u32[]{:S(2)}) copy-start(s32[1,8]{1,0:T(1,128)} %refs_2_.5) | copy-start | bytes 100
  2.5 4.7 %collective-permute-start.2 = (bf16[272,256]{1,0:T(8,128)(2,1)S(1)}, bf16[272,256]{1,0:T(8,128)(2,1)S(1)}, u32[]{:S(2)}, u32[]{:S(2)}) collective-permute-start(bf16[272,256]{1,0:T(8,128)(2,1)S(1)} %fusion.1), channel_id=1, source_target_pairs={{0,2},{2,0},{4,6},{6,4},{8,10},{10,8},{12,14},{14,12},{16,18},{18,... | collective-permute-start | bytes 417800 | tf_op jit(solution)/shard_map/ppermute | solution.py:410
  5.1 31.9 %collective-permute-start.3 = (bf16[256,1024]{1,0:T(8,128)(2,1)}, bf16[256,1024]{1,0:T(8,128)(2,1)S(1)}, u32[]{:S(2)}, u32[]{:S(2)}) collective-permute-start(bf16[256,1024]{1,0:T(8,128)(2,1)} %constant_dynamic-slice_fusion.2), channel_id=1, source_target_pairs={{0,2},{2,0},{4,6},{6,4},{8,10},{10,8},{12,14},{14,12},{16,18},{18,... | collective-permute-start | bytes 1572872 | tf_op jit(solution)/shard_map/ppermute | solution.py:410
  5.8 4.0 %collective-permute-start = (bf16[128,512]{1,0:T(8,128)(2,1)}, bf16[128,512]{1,0:T(8,128)(2,1)}, u32[]{:S(2)}, u32[]{:S(2)}) collective-permute-start(bf16[128,512]{1,0:T(8,128)(2,1)} %pad_maximum_fusion.1), channel_id=1, source_target_pairs={{0,2},{2,4},{4,6},{6,8},{8,10},{10,12},{12,14},{14,16},{16,18},{18... | collective-permute-start | bytes 393224 | tf_op jit(solution)/shard_map/ppermute | solution.py:405
  7.2 25.6 %collective-permute-start.5 = (bf16[512,256]{1,0:T(8,128)(2,1)S(1)}, bf16[512,256]{1,0:T(8,128)(2,1)S(1)}, u32[]{:S(2)}, u32[]{:S(2)}) collective-permute-start(bf16[512,256]{1,0:T(8,128)(2,1)S(1)} %pad_maximum_fusion.refs_7_), channel_id=1, source_target_pairs={{0,8},{2,10},{4,12},{6,14},{8,16},{10,18},{12,20},{14,22},{16,24},... | collective-permute-start | bytes 786440 | tf_op jit(solution)/shard_map/ppermute | solution.py:405
  8.5 24.3 %collective-permute-start.7 = (bf16[512,256]{1,0:T(8,128)(2,1)S(1)}, bf16[512,256]{1,0:T(8,128)(2,1)S(1)}, u32[]{:S(2)}, u32[]{:S(2)}) collective-permute-start(bf16[512,256]{1,0:T(8,128)(2,1)S(1)} %pad_maximum_fusion.refs_7_), channel_id=1, source_target_pairs={{0,16},{2,18},{4,20},{6,22},{8,24},{10,26},{12,28},{14,30},{1,17},... | collective-permute-start | bytes 786440 | tf_op jit(solution)/shard_map/ppermute | solution.py:405
  9.9 0.9 copy-start.2
  10.8 0.9 copy-start.3
  11.7 0.7 copy-start.7
  29.2 113.1 %collective-permute-start.1 = (bf16[128,2048]{1,0:T(8,128)(2,1)}, bf16[128,2048]{1,0:T(8,128)(2,1)}, u32[]{:S(2)}, u32[]{:S(2)}) collective-permute-start(bf16[128,2048]{1,0:T(8,128)(2,1)} %get-tuple-element.13), channel_id=1, source_target_pairs={{0,1},{1,0},{2,3},{3,2},{4,5},{5,4},{6,7},{7,6},{8,9},{9,8},{10,11... | collective-permute-start | bytes 1572872 | tf_op jit(solution)/shard_map/ppermute | solution.py:455
  30.4 6.5 %collective-permute-start.4 = (bf16[512,256]{1,0:T(8,128)(2,1)S(1)}, bf16[512,256]{1,0:T(8,128)(2,1)S(1)}, u32[]{:S(2)}, u32[]{:S(2)}) collective-permute-start(bf16[512,256]{1,0:T(8,128)(2,1)S(1)} %pad_maximum_fusion.refs_7_), channel_id=1, source_target_pairs={{0,4},{2,6},{4,0},{6,2},{8,12},{10,14},{12,8},{14,10},{16,20},{18,... | collective-permute-start | bytes 786440 | tf_op jit(solution)/shard_map/ppermute | solution.py:410
  32.8 28.4 %collective-permute-start.6 = (bf16[512,256]{1,0:T(8,128)(2,1)S(1)}, bf16[512,256]{1,0:T(8,128)(2,1)S(1)}, u32[]{:S(2)}, u32[]{:S(2)}) collective-permute-start(bf16[512,256]{1,0:T(8,128)(2,1)S(1)} %collective-permute-done.5.refs_9_), channel_id=1, source_target_pairs={{0,4},{2,6},{4,0},{6,2},{8,12},{10,14},{12,8},{14,10},{16,20},{18,... | collective-permute-start | bytes 786440 | tf_op jit(solution)/shard_map/ppermute | solution.py:410
  32.8 45.2 %collective-permute-start.8 = (bf16[512,256]{1,0:T(8,128)(2,1)S(1)}, bf16[512,256]{1,0:T(8,128)(2,1)S(1)}, u32[]{:S(2)}, u32[]{:S(2)}) collective-permute-start(bf16[512,256]{1,0:T(8,128)(2,1)S(1)} %collective-permute-done.7.refs_8_.refs_11_), channel_id=1, source_target_pairs={{0,4},{2,6},{4,0},{6,2},{8,12},{10,14},{12,8},{14,10},{16,20},{18,... | collective-permute-start | bytes 786440 | tf_op jit(solution)/shard_map/ppermute | solution.py:410
  37.0 0.7 copy-start.6
  133.2 0.7 copy-start.8
  134.0 0.7 copy-start.9
  134.7 9.5 %collective-permute-start.9 = (bf16[128,1024]{1,0:T(8,128)(2,1)}, bf16[128,1024]{1,0:T(8,128)(2,1)S(1)}, u32[]{:S(2)}, u32[]{:S(2)}) collective-permute-start(bf16[128,1024]{1,0:T(8,128)(2,1)} %get-tuple-element.19), channel_id=1, source_target_pairs={{0,1},{1,0},{2,3},{3,2},{4,5},{5,4},{6,7},{7,6},{8,9},{9,8},{10,11... | collective-permute-start | bytes 786440 | tf_op jit(solution)/shard_map/ppermute | solution.py:472
  134.9 10.0 %collective-permute-start.10 = (bf16[128,1024]{1,0:T(8,128)(2,1)}, bf16[128,1024]{1,0:T(8,128)(2,1)S(1)}, u32[]{:S(2)}, u32[]{:S(2)}) collective-permute-start(bf16[128,1024]{1,0:T(8,128)(2,1)} %copy-done.9), channel_id=1, source_target_pairs={{0,2},{1,3},{2,0},{3,1},{4,6},{5,7},{6,4},{7,5},{8,10},{9,11},{10,... | collective-permute-start | bytes 786440 | tf_op jit(solution)/shard_map/ppermute | solution.py:472
  141.1 10.9 %collective-permute-start.11 = (bf16[128,1024]{1,0:T(8,128)(2,1)}, bf16[128,1024]{1,0:T(8,128)(2,1)S(1)}, u32[]{:S(2)}, u32[]{:S(2)}) collective-permute-start(bf16[128,1024]{1,0:T(8,128)(2,1)} %copy-done.8), channel_id=1, source_target_pairs={{0,3},{1,2},{2,1},{3,0},{4,7},{5,6},{6,5},{7,4},{8,11},{9,10},{10,... | collective-permute-start | bytes 786440 | tf_op jit(solution)/shard_map/ppermute | solution.py:472

commit v2 on v1

v2 whole, which is shorter than its diff:
```python
import functools
import jax
import jax.numpy as jnp
from jax import lax
from jax.experimental import pallas as pl
from jax.experimental.pallas import tpu as pltpu
from jax.sharding import PartitionSpec as P

HD = 64
G = 8
WIN = 128
BACK = 8
LOG2E = 1.4426950408889634
SCORE_SCALE = HD ** (-0.5) * LOG2E
NEG = -1e30
SAFE_TOTAL = 2.0**100
NEVER = 2**30
FEATURES = 128
SHARD_LANE = 64
CUT = 2.0**15
TALL = HD + 16
PARAMS = pltpu.CompilerParams(
    dimension_semantics=("arbitrary",), vmem_limit_bytes=48 * 1024 * 1024
)


def interval_rows(starts_ref):
    lane = lax.broadcasted_iota(jnp.int32, (8, FEATURES), 1)
    begin = jnp.full((8, FEATURES), NEVER, jnp.int32)
    end = begin
    for i in range(starts_ref.shape[0]):
        entry = starts_ref[i]
        begin = jnp.where(lane == i, entry, begin)
        end = jnp.where(lane == i - 1, entry, end)
    return begin, end


def key_features(starts_ref, low, shard, rows):
    begin, end = interval_rows(starts_ref)
    u = low + lax.broadcasted_iota(jnp.int32, (rows, FEATURES), 0)
    lane = lax.broadcasted_iota(jnp.int32, (rows, FEATURES), 1)
    own = jnp.where(shard < 0, SHARD_LANE - 1, SHARD_LANE + shard)
    marked = (lane == own) | ((u >= begin[:1]) & (u < end[:1]))
    return jnp.where(marked, 1.0, 0.0).astype(jnp.bfloat16)


def query_features(starts_ref, low, named, rows):
    begin, end = (x.T[:, :1] for x in interval_rows(starts_ref))
    t = low + lax.broadcasted_iota(jnp.int32, (FEATURES, rows), 1)
    row = lax.broadcasted_iota(jnp.int32, (FEATURES, rows), 0)
    seen = (t >= begin) & (t < end) & (row < SHARD_LANE)
    for shard in named:
        seen = seen | ((row == SHARD_LANE + shard) & (shard >= 0))
    return jnp.where(seen, 0.0, -CUT).astype(jnp.bfloat16)


def score(key_block, query_cols):
    return jnp.dot(key_block, query_cols, preferred_element_type=jnp.float32) * SCORE_SCALE


def plain_weights(key_block, query_cols, bias=None):
    scores = score(key_block, query_cols)
    if bias is not None:
        scores = scores + bias
    return jnp.exp2(scores).astype(jnp.bfloat16)


def weigh(value_rows, weight):
    return jnp.dot(value_rows, weight, preferred_element_type=jnp.float32)


def topped(state, key_block, query_cols, value_rows, bias=None):
    top, acc = state
    scores = score(key_block, query_cols)
    if bias is not None:
        scores = scores + bias
    new_top = jnp.maximum(top, jnp.max(scores, axis=0, keepdims=True))
    weight = jnp.exp2(scores - new_top).astype(jnp.bfloat16)
    return new_top, acc * jnp.exp2(top - new_top) + weigh(value_rows, weight)


def fresh(total):
    row = lax.broadcasted_iota(jnp.int32, (TALL, total.shape[1]), 0)
    return jnp.where(row == HD, total, 0.0)


def slotted(col, head, heads):
    if heads == 1:
        return col
    empty = jnp.zeros_like(col)
    return jnp.concatenate([jnp.where(head == i, col, empty) for i in range(heads)], axis=0)


def overflowed(total):
    return jnp.max(jnp.where(total <= SAFE_TOTAL, 0.0, 1.0)) > 0.5


def sink_lanes(sink_ref, first, count, rows):
    return jnp.concatenate(
        [jnp.full((1, rows), sink_ref[first + e] * LOG2E, jnp.float32) for e in range(count)], axis=1
    )


class DocPlan:
    def __init__(self, first, last, grp, heads, earlier, units, rows, pieces, wide=4):
        self.first, self.last, self.grp, self.heads = first, last, grp, heads
        self.earlier, self.units, self.rows, self.pieces = earlier, units, rows, pieces
        self.wide = wide


def doc_body(plan, *refs):
    first, last, grp, heads, rows = plan.first, plan.last, plan.grp, plan.heads, plan.rows
    wide = plan.wide
    count = plan.earlier + plan.units
    refs = list(refs)
    where_ref, starts_ref, sink_ref = refs[:3]
    del refs[:3]
    list_refs = [refs.pop(0) for _ in range(grp)]
    query_refs = [refs.pop(0) for _ in range(grp)]
    unit_refs = [refs.pop(0) for _ in range(count)]
    if not first:
        acc_in = refs.pop(0)
    if last:
        piece_refs = [refs.pop(0) for _ in range(2 * grp if plan.pieces else 1)]
    else:
        acc_out = refs.pop(0)
    value_ref, key_ref, bias_ref, acc_ref, cols_ref = refs
    step = pl.program_id(0)
    core = where_ref[1]
    lowest = where_ref[0] - core
    width = heads * HD
    part = wide * rows
    lanes = grp * part
    new = range(plan.earlier, count)
    own = 0 if first or plan.earlier else -1

    def set_unit(n):
        unit = unit_refs[n][...]
        turned = unit[:, width:].T if width % 128 == 0 else unit.T[width:]
        for i in range(heads):
            value_ref[n, i, :HD] = turned[i * HD : (i + 1) * HD]
            value_ref[n, i, HD:] = jnp.ones((TALL - HD, grp * rows), jnp.bfloat16)
        key_ref[n, :, FEATURES:] = unit[:, :width]
        for r in range(grp):
            shard = lowest + (r ^ core) - where_ref[4 + n] if grp > 1 else lowest - where_ref[4 + n]
            marks = key_features(starts_ref, shard * rows, shard, rows)
            key_ref[n, r * rows : (r + 1) * rows, :FEATURES] = marks

    @pl.when(step == 0)
    def _():
        for n in new:
            set_unit(n)
        for a in range(grp):
            entries = [list_refs[0][0, i] for i in range(BACK)]
            if grp == 2:
                entries = [jnp.where(core == a, x, list_refs[1][0, i]) for i, x in enumerate(entries)]
            named = [lowest + a] + entries
            marks = query_features(starts_ref, (lowest + a) * rows, named, rows)
            for e in range(wide):
                spot = slice(a * part + e * rows, a * part + (e + 1) * rows)
                cols_ref[:FEATURES, spot] = marks
        if own == 0:
            u = lax.broadcasted_iota(jnp.int32, (rows, part), 0)
            t = jnp.bitwise_and(lax.broadcasted_iota(jnp.int32, (rows, part), 1), rows - 1)
            bias_ref[...] = jnp.where(u <= t, 0.0, NEG)

    head = step // (G // wide)
    sinks = sink_lanes(sink_ref, core * heads * G + wide * step, wide, rows)
    sinks = jnp.concatenate([sinks] * grp, axis=1)
    for a in range(grp):
        query = query_refs[0][...]
        if grp == 2:
            query = jnp.where(core == a, query, query_refs[1][...])
        turned = query.T
        for e in range(wide):
            spot = slice(a * part + e * rows, a * part + (e + 1) * rows)
            cols_ref[FEATURES:, spot] = slotted(turned[e * HD : (e + 1) * HD], head, heads)

    def own_span(r):
        return slice(0, rows) if grp == 1 else pl.ds(pl.multiple_of((r ^ core) * rows, rows), rows)

    def own_pairs():
        pairs = [(r, slice(r * part, (r + 1) * part), bias_ref[...]) for r in range(grp)]
        return pairs + ([(0, slice(part, lanes), None)] if grp == 2 else [])

    def rows_of(n):
        return [slice(r * rows, (r + 1) * rows) for r in range(grp)]

    gain = fresh(jnp.exp2(sinks)) if first else acc_in[0]
    gains = [gain[:, a * part : (a + 1) * part] for a in range(grp)]
    for n in new:
        if n == own:
            for r, span, bias in own_pairs():
                weight = plain_weights(key_ref[n, own_span(r)], cols_ref[:, span], bias)
                a = span.start // part
                gains[a] = gains[a] + weigh(value_ref[n, head, :, own_span(r)], weight)
            continue
        for a in range(grp):
            cols = cols_ref[:, a * part : (a + 1) * part]
            weights = [plain_weights(key_ref[n, span], cols) for span in rows_of(n)]
            gains[a] = gains[a] + weigh(value_ref[n, head], jnp.concatenate(weights, axis=0))
    for a in range(grp):
        acc_ref[:, a * part : (a + 1) * part] = gains[a]

    if not last:
        acc_out[0] = acc_ref[...]
        return

    @pl.when(overflowed(acc_ref[HD : HD + 1]))
    def _():
        for n in range(plan.earlier):
            set_unit(n)
        for a in range(grp):
            spot = slice(a * part, (a + 1) * part)
            state = sinks[:, spot], fresh(jnp.ones((1, part), jnp.float32))
            for r, span, bias in own_pairs():
                if span.start == a * part:
                    values = value_ref[0, head, :, own_span(r)]
                    state = topped(state, key_ref[0, own_span(r)], cols_ref[:, spot], values, bias)
            for n in range(1, count):
                for span in rows_of(n):
                    values = value_ref[n, head, :, span]
                    state = topped(state, key_ref[n, span], cols_ref[:, spot], values)
            acc_ref[:, spot] = state[1]

    result = acc_ref[:HD] * (1.0 / acc_ref[HD : HD + 1])
    blocks = []
    for a in range(grp):
        parts = [result[:, a * part + e * rows : a * part + (e + 1) * rows] for e in range(wide)]
        blocks.append(jnp.concatenate(parts, axis=0).T.astype(jnp.bfloat16))
    if not plan.pieces:
        piece_refs[0][...] = blocks[0]
        return
    half = rows // 2
    side = where_ref[2]
    for a in range(grp):
        block = jnp.where(core == a, blocks[0], blocks[1])
        low, high = block[:half], block[half:]
        piece_refs[2 * a][...] = jnp.where(side == 0, low, high)
        piece_refs[2 * a + 1][...] = jnp.where(side == 0, high, low)


def doc_call(plan, where, starts, sinks, lists, queries, units, state, columns):
    grp, heads, rows, wide = plan.grp, plan.heads, plan.rows, plan.wide
    steps = heads * G // wide
    size = wide * HD
    width = heads * HD
    count = plan.earlier + plan.units
    smem = pl.BlockSpec(memory_space=pltpu.SMEM)
    args = [where, starts, sinks, *lists]
    specs = [smem] * (2 + grp)
    args += list(queries)
    specs.append(pl.BlockSpec((rows, size), lambda j, w: (0, w[1] * steps + j)))
    if grp == 2:
        specs.append(pl.BlockSpec((rows, size), lambda j, w: (0, j)))
    for unit in units:
        args.append(unit)
        specs.append(pl.BlockSpec((grp * rows, 2 * width), lambda j, w: (0, 0)))
    lanes = wide * grp * rows
    state_spec = pl.BlockSpec((1, TALL, lanes), lambda j, w: (j, 0, 0))
    aliases = {}
    if not plan.first:
        if not plan.last:
            aliases = {len(args): 0}
        args.append(state)
        specs.append(state_spec)
    if not plan.last:
        out_shape = [jax.ShapeDtypeStruct((steps, TALL, lanes), jnp.float32)]
        out_specs = [state_spec]
    elif plan.pieces:
        half = rows // 2
        out_shape = [jax.ShapeDtypeStruct((half, columns), jnp.bfloat16)]
        out_specs = [pl.BlockSpec((half, size), lambda j, w: (0, w[3] * steps + j))]
        for _ in range(2 * grp - 1):
            out_shape.append(jax.ShapeDtypeStruct((half, steps * size), jnp.bfloat16))
            out_specs.append(pl.BlockSpec((half, size), lambda j, w: (0, j)))
    else:
        out_shape = [jax.ShapeDtypeStruct((rows, steps * size), jnp.bfloat16)]
        out_specs = [pl.BlockSpec((rows, size), lambda j, w: (0, j))]
    return pl.pallas_call(
        functools.partial(doc_body, plan),
        out_shape=out_shape,
        grid_spec=pltpu.PrefetchScalarGridSpec(
            num_scalar_prefetch=1,
            grid=(steps,),
            in_specs=specs,
            out_specs=out_specs,
            scratch_shapes=[
                pltpu.VMEM((count, heads, TALL, grp * rows), jnp.bfloat16),
                pltpu.VMEM((count, grp * rows, FEATURES + width), jnp.bfloat16),
                pltpu.VMEM((rows, wide * rows), jnp.float32),
                pltpu.VMEM((TALL, lanes), jnp.float32),
                pltpu.VMEM((FEATURES + width, lanes), jnp.bfloat16),
            ],
        ),
        input_output_aliases=aliases,
        compiler_params=PARAMS,
        name="doc_attention",
    )(*args)


def band_body(heads, rows, wide, pieces, where_ref, starts_ref, sink_ref, query_ref, key_ref, value_ref, rim_ref, *refs):
    out_refs, (keys, values, bias_ref, cols_ref, acc_ref) = refs[:-5], refs[-5:]
    step = pl.program_id(0)
    width = heads * HD
    low = where_ref[0] * rows
    tiles = rows // WIN
    lanes = wide * WIN

    @pl.when(step == 0)
    def _():
        rim = rim_ref[...]
        keys[:WIN, FEATURES:] = rim[:, :width]
        keys[WIN:, FEATURES:] = key_ref[...]
        shard = where_ref[0]
        keys[:WIN, :FEATURES] = key_features(starts_ref, low - WIN, shard - 1, WIN)
        keys[WIN:, :FEATURES] = key_features(starts_ref, low, shard, rows)
        turned_rim = rim[:, width:].T if width % 128 == 0 else rim.T[width:]
        turned_own = value_ref[...].T
        for i in range(heads):
            values[i, :HD, :WIN] = turned_rim[i * HD : (i + 1) * HD]
            values[i, :HD, WIN:] = turned_own[i * HD : (i + 1) * HD]
            values[i, HD:] = jnp.ones((TALL - HD, rows + WIN), jnp.bfloat16)
        marks = query_features(starts_ref, low, [shard, shard - 1], rows)
        for tile in range(tiles):
            for e in range(wide):
                cols_ref[tile, :FEATURES, e * WIN : (e + 1) * WIN] = marks[:, tile * WIN : (tile + 1) * WIN]
        u = lax.broadcasted_iota(jnp.int32, (2 * WIN, lanes), 0)
        t = jnp.bitwise_and(lax.broadcasted_iota(jnp.int32, (2 * WIN, lanes), 1), WIN - 1)
        bias_ref[...] = jnp.where((u <= t + WIN) & (u > t), 0.0, NEG)

    head = step // (G // wide)
    turned = query_ref[...].T
    sinks = sink_lanes(sink_ref, wide * step, wide, WIN)

    for tile in range(tiles):
        span = slice(tile * WIN, (tile + 1) * WIN)
        for e in range(wide):
            col = slotted(turned[e * HD : (e + 1) * HD, span], head, heads)
            cols_ref[tile, FEATURES:, e * WIN : (e + 1) * WIN] = col
    for tile in range(tiles):
        span = slice(tile * WIN, (tile + 2) * WIN)
        weight = plain_weights(keys[span], cols_ref[tile], bias_ref[...])
        acc_ref[tile] = fresh(jnp.exp2(sinks)) + weigh(values[head, :, span], weight)

    @pl.when(overflowed(acc_ref[:, HD : HD + 1]))
    def _():
        for tile in range(tiles):
            span = slice(tile * WIN, (tile + 2) * WIN)
            state = sinks, fresh(jnp.ones((1, lanes), jnp.float32))
            state = topped(state, keys[span], cols_ref[tile], values[head, :, span], bias_ref[...])
            acc_ref[tile] = state[1]

    finished = []
    for tile in range(tiles):
        result = acc_ref[tile, :HD] * (1.0 / acc_ref[tile, HD : HD + 1])
        parts = [result[:, e * WIN : (e + 1) * WIN] for e in range(wide)]
        finished.append(jnp.concatenate(parts, axis=0).T.astype(jnp.bfloat16))
    if pieces:
        side = where_ref[2]
        out_refs[0][...] = jnp.where(side == 0, finished[0], finished[1])
        out_refs[1][...] = jnp.where(side == 0, finished[1], finished[0])
    else:
        for tile, value in enumerate(finished):
            out_refs[0][tile * WIN : (tile + 1) * WIN] = value


def band_call(where, starts, sinks, queries, keys, value_rows, rim, heads, rows, pieces, columns):
    wide = 4
    steps = heads * G // wide
    size = wide * HD
    width = heads * HD
    tiles = rows // WIN
    smem = pl.BlockSpec(memory_space=pltpu.SMEM)
    if pieces:
        out_shape = [
            jax.ShapeDtypeStruct((WIN, columns), jnp.bfloat16),
            jax.ShapeDtypeStruct((WIN, steps * size), jnp.bfloat16),
        ]
        out_specs = [
            pl.BlockSpec((WIN, size), lambda j, w: (0, w[2] * steps + j)),
            pl.BlockSpec((WIN, size), lambda j, w: (0, j)),
        ]
    else:
        out_shape = [jax.ShapeDtypeStruct((rows, steps * size), jnp.bfloat16)]
        out_specs = [pl.BlockSpec((rows, size), lambda j, w: (0, j))]

    def fixed(j, w):
        return (0, 0)

    return pl.pallas_call(
        functools.partial(band_body, heads, rows, wide, pieces),
        out_shape=out_shape,
        grid_spec=pltpu.PrefetchScalarGridSpec(
            num_scalar_prefetch=1,
            grid=(steps,),
            in_specs=[
                smem,
                smem,
                pl.BlockSpec((rows, size), lambda j, w: (0, j)),
                pl.BlockSpec((rows, width), fixed),
                pl.BlockSpec((rows, width), fixed),
                pl.BlockSpec((WIN, 2 * width), fixed),
            ],
            out_specs=out_specs,
            scratch_shapes=[
                pltpu.VMEM((rows + WIN, FEATURES + width), jnp.bfloat16),
                pltpu.VMEM((heads, TALL, rows + WIN), jnp.bfloat16),
                pltpu.VMEM((2 * WIN, wide * WIN), jnp.float32),
                pltpu.VMEM((tiles, FEATURES + width, wide * WIN), jnp.bfloat16),
                pltpu.VMEM((tiles, TALL, wide * WIN), jnp.float32),
            ],
        ),
        compiler_params=PARAMS,
        name="band_attention",
    )(where, starts, sinks, queries, keys, value_rows, rim)


def shifted(value, steps):
    count = lax.axis_size("seq")
    return lax.ppermute(value, "seq", [(i, i + steps) for i in range(count - steps)])


def swapped(value, bit):
    count = lax.axis_size("seq")
    return lax.ppermute(value, "seq", [(i, i ^ bit) for i in range(count)])


def relay(result):
    return lax.all_to_all(result, "kv", split_axis=0, concat_axis=1, tiled=True)


def paired_program(
    q_band, k_band, v_band, sink_band, q_doc, k_doc, v_doc, sink_doc, doc_starts, source_lists
):
    rows = q_band.shape[0]
    heads = k_band.shape[1] // HD
    mine = heads // 2
    width = mine * HD
    columns = 2 * q_band.shape[1]
    shard, side = lax.axis_index("seq"), lax.axis_index("kv")
    core = shard % 2
    layer = shard // 2 % 2
    flip = 4 * layer - 2

    def place(*dists):
        return jnp.stack([shard, core, side, 2 * side + core, *dists]).astype(jnp.int32)

    def half(value, which, size):
        return lax.dynamic_slice_in_dim(value, which * size, size, axis=1)

    away = jnp.concatenate([half(k_doc, 1 - core, width), half(v_doc, 1 - core, width)], axis=1)
    near = swapped(away, 1)
    rim = jnp.concatenate([k_band[rows - WIN :], v_band[rows - WIN :]], axis=1)
    rim = shifted(rim, 1)
    kept = jnp.concatenate([half(k_doc, core, width), half(v_doc, core, width)], axis=1)
    unit = jnp.concatenate([kept, near], axis=0)
    back4 = shifted(unit, 4)
    back8 = shifted(unit, 8)
    q_later, _ = lax.optimization_barrier((q_doc, unit))
    mate_lists = swapped(source_lists, 1)
    q_mate = swapped(half(q_later, 1 - core, mine * G * HD), 1)
    cross4 = swapped(back4, 2)
    late = swapped(jnp.where(layer == 0, unit, back8), 2)
    band_out, band_send = band_call(
        place(), doc_starts, sink_band, q_band, k_band, v_band, rim, heads, rows, True, columns
    )
    band_got = lax.ppermute(band_send, "kv", [(0, 1), (1, 0)])
    out_band = lax.dynamic_update_slice(band_out, band_got, (0, (1 - side) * q_band.shape[1]))

    def doc(first, last, units, dists, earlier, state):
        plan = DocPlan(first, last, 2, mine, earlier, len(units) - earlier, rows, True)
        return doc_call(
            plan, place(*dists), doc_starts, sink_doc, (source_lists, mate_lists),
            (q_doc, q_mate), units, state, columns,
        )

    units = [unit, back4, cross4, back8, late]
    dists = [0, 4, 4 + flip, 8, jnp.where(layer == 0, 6, 2)]
    (state,) = doc(True, False, units[:2], dists[:2], 0, None)
    (state,) = doc(False, False, units[2:4], dists[2:4], 0, state)
    out_doc, *sends = doc(False, True, units, dists, 4, state)
    size = mine * G * HD
    for mask, send in zip((1, 2, 3), sends):
        count = 2 * lax.axis_size("seq")
        got = lax.ppermute(send, ("seq", "kv"), [(i, i ^ mask) for i in range(count)])
        source = ((2 * side + core) ^ (mask & 1) * 2 ^ (mask >> 1)) * size
        out_doc = lax.dynamic_update_slice(out_doc, got, (0, source))
    return out_band, out_doc


def plain_program(
    q_band, k_band, v_band, sink_band, q_doc, k_doc, v_doc, sink_doc, doc_starts, source_lists
):
    rows = q_band.shape[0]
    heads = k_band.shape[1] // HD
    shard = lax.axis_index("seq")

    def place(*dists):
        return jnp.stack([shard, 0, 0, 0, *dists]).astype(jnp.int32)

    rim = jnp.concatenate([k_band[rows - WIN :], v_band[rows - WIN :]], axis=1)
    rim = shifted(rim, 1)
    unit = jnp.concatenate([k_doc, v_doc], axis=1)
    units = [unit] + [shifted(unit, d) for d in range(1, BACK + 1)]
    band = band_call(
        place(), doc_starts, sink_band, q_band, k_band, v_band, rim, heads, rows, False, None
    )[0]
    plan = DocPlan(True, True, 1, heads, 0, BACK + 1, rows, False)
    doc = doc_call(
        plan, place(*range(BACK + 1)), doc_starts, sink_doc, (source_lists,),
        (q_doc,), units, None, None,
    )[0]
    return relay(band), relay(doc)


def solution(mesh):
    placed = (
        P("seq", "kv"),
        P("seq", "kv"),
        P("seq", "kv"),
        P("kv"),
        P("seq", "kv"),
        P("seq", "kv"),
        P("seq", "kv"),
        P("kv"),
        P(),
        P("seq", None),
    )

    def per_device(*args):
        heads = args[1].shape[1] // HD
        even = heads % 4 == 0 and mesh.shape["kv"] == 2 and mesh.shape["seq"] % 4 == 0
        return (paired_program if even else plain_program)(*args)

    return jax.shard_map(
        per_device,
        mesh=mesh,
        in_specs=placed,
        out_specs=(P(("seq", "kv"), None), P(("seq", "kv"), None)),
        check_vma=False,
    )
```

time: 153 us -> 139 us (0.908)
  the two profiles are of different devices: /device:TPU:27 before, /device:TPU:17 now
where the time goes in v2:
time: 139 us; the launch traced here: 138 us
  Pallas kernels  86.6 us (62%)
  starting transfers between devices  27.7 us (20%)
  local copies, waits for them, and re-layouts  12 us (9%)
  waiting for transfers between devices  9.41 us (7%)
  other arithmetic  1.81 us (1%)
    pallas_call x3, Pallas kernels, doc_call(): pl.pallas_call(functools.partial(doc_body, plan), out_shape=out_shape, gr...  67.6 us
    pallas_call x1, Pallas kernels, band_call(): pl.pallas_call(functools.partial(band_body, heads, rows, wide, pieces), o...  19 us
    ppermute x5, starting transfers between devices, swapped(): return lax.ppermute(value, 'seq', [(i, i ^ bit) for i in range(count)])  16.7 us
    ppermute x3, waiting for transfers between devices, paired_program(): lax.ppermute(send, ('seq', 'kv'), [(i, i ^ mask) for i in range(count)])  8.55 us
    ppermute x3, starting transfers between devices, shifted(): lax.ppermute(value, 'seq', [(i, i + steps) for i in range(count - steps)])  7.79 us
    unnamed x24, local copies, waits for them, and re-layouts  3.09 us
    dynamic_slice x2, local copies, waits for them, and re-layouts, half(): return lax.dynamic_slice_in_dim(value, which * size, size, axis=1)  2.98 us
  transfers between devices with their start and end apart: 12, of which 4 were waited for; matrix products, arithmetic and copies ran while one was open for 6% of the time, Pallas kernels for 63%

profile of v2, /device:TPU:17, one launch (start us, length us, event | category | flops | bytes accessed | tf_op | source)
XLA Modules:
  0.0 138.4 jit_solution(14687055196128558892)
XLA Ops:
  0.7 1.1 constant_dynamic-slice_fusion.3
  1.9 0.7 collective-permute-start.3
  2.6 0.8 slice.6
  3.5 0.8 slice.7
  4.4 3.2 %collective-permute-start.5 = (bf16[512,256]{1,0:T(8,128)(2,1)S(1)}, bf16[512,256]{1,0:T(8,128)(2,1)S(1)}, u32[]{:S(2)}, u32[]{:S(2)}) collective-permute-start(bf16[512,256]{1,0:T(8,128)(2,1)S(1)} %pad_maximum_fusion.refs_7_), channel_id=1, source_target_pairs={{0,8},{2,10},{4,12},{6,14},{8,16},{10,18},{12,20},{14,22},{16,24},... | collective-permute-start | bytes 786440 | tf_op jit(solution)/shard_map/ppermute | solution.py:421
  7.6 1.3 collective-permute-start.7
  9.6 3.3 %collective-permute-start = (bf16[128,512]{1,0:T(8,128)(2,1)}, bf16[128,512]{1,0:T(8,128)(2,1)}, u32[]{:S(2)}, u32[]{:S(2)}) collective-permute-start(bf16[128,512]{1,0:T(8,128)(2,1)} %pad_maximum_fusion.1), channel_id=1, source_target_pairs={{0,2},{2,4},{4,6},{6,8},{8,10},{10,12},{12,14},{14,16},{16,18},{18... | collective-permute-start | bytes 393224 | tf_op jit(solution)/shard_map/ppermute | solution.py:421
  12.9 1.9 %constant_dynamic-slice_fusion = bf16[256,1024]{1,0:T(8,128)(2,1)} fusion(bf16[256,2048]{1,0:T(8,128)(2,1)} %refs_5_.5, s32[]{:T(128)S(6)} %select_n.57), kind=kLoop, calls=%fused_computation.7 | loop fusion | bytes 1048580 | tf_op jit(solution)/shard_map/dynamic_slice | solution.py:450
  15.1 0.9 copy-done.4
  16.7 19.0 %band_attention.1 = (bf16[128,4096]{1,0:T(8,128)(2,1)}, bf16[128,2048]{1,0:T(8,128)(2,1)}) custom-call(s32[4]{0:T(128)S(1)} %pad_add_fusion.where_ref, s32[16]{0:T(128)S(1)} %copy-done.5, f32[32]{0:T(128)S(1)} %copy-done.8, bf16[256,2048]{1,0:T(8,128)(2,1)S(1)} %copy-done.2, bf16[256,256]{1,0:T(8,128)(2,1)S(1)} %copy-done.3, bf16[256,256]{1,0:T(8,128)(2,1)S(1)} %copy-done.4, ...), custom_call_target="tpu_custom_call" | custom-call | tf_op jit(solution)/shard_map/band_attention/pallas_call | solution.py:391
  35.7 1.2 collective-permute-start.1
  36.9 1.5 %collective-permute-start.6 = (bf16[512,256]{1,0:T(8,128)(2,1)S(1)}, bf16[512,256]{1,0:T(8,128)(2,1)S(1)}, u32[]{:S(2)}, u32[]{:S(2)}) collective-permute-start(bf16[512,256]{1,0:T(8,128)(2,1)S(1)} %collective-permute-done.5.refs_8_), channel_id=1, source_target_pairs={{0,4},{2,6},{4,0},{6,2},{8,12},{10,14},{12,8},{14,10},{16,20},{18,... | collective-permute-start | bytes 786440 | tf_op jit(solution)/shard_map/ppermute | solution.py:426
  38.4 1.0 broadcast_select_fusion
  39.5 14.3 %collective-permute-start.2 = (s32[1,8]{1,0:T(1,128)S(1)}, s32[1,8]{1,0:T(1,128)S(1)}, u32[]{:S(2)}, u32[]{:S(2)}) collective-permute-start(s32[1,8]{1,0:T(1,128)S(1)} %copy-done.7), channel_id=1, source_target_pairs={{0,2},{2,0},{4,6},{6,4},{8,10},{10,8},{12,14},{14,12},{16,18},{18,... | collective-permute-start | bytes 104 | tf_op jit(solution)/shard_map/ppermute | solution.py:426
  54.7 10.8 %doc_attention.3.refs_9_ = f32[4,80,2048]{2,1,0:T(8,128)S(1)} custom-call(s32[6]{0:T(128)S(1)} %stack.52.refs_0_, s32[16]{0:T(128)S(1)} %copy-done.5, f32[32]{0:T(128)S(1)} %copy-done.6, s32[1,8]{1,0:T(1,128)S(1)} %copy-done.7, s32[1,8]{1,0:T(1,128)S(1)} %collective-permute-done.2.refs_4_, bf16[256,2048]{1,0:T(8,128)(2,1)S(1)} %copy-done.1, ...), custom_call_target="tpu_custom_call" | custom-call | tf_op jit(solution)/shard_map/doc_attention/pallas_call | solution.py:280
  65.5 10.5 %doc_attention.4.refs_12_ = f32[4,80,2048]{2,1,0:T(8,128)S(1)} custom-call(s32[6]{0:T(128)S(1)} %stack.51.refs_0_, s32[16]{0:T(128)S(1)} %copy-done.5, f32[32]{0:T(128)S(1)} %copy-done.6, s32[1,8]{1,0:T(1,128)S(1)} %copy-done.7, s32[1,8]{1,0:T(1,128)S(1)} %collective-permute-done.2.refs_4_, ...), custom_call_target="tpu_custom_call", output_to_operand_aliasing={{}: (9, {})} | custom-call | tf_op jit(solution)/shard_map/doc_attention/pallas_call | solution.py:280
  76.1 1.5 %copy-done = f32[4,80,2048]{2,1,0:T(8,128)} copy-done((f32[4,80,2048]{2,1,0:T(8,128)}, f32[4,80,2048]{2,1,0:T(8,128)S(1)}, u32[]{:S(2)}) %copy-start) | copy-done | bytes 2621464
  77.6 46.2 %doc_attention.5 = (bf16[128,4096]{1,0:T(8,128)(2,1)}, bf16[128,1024]{1,0:T(8,128)(2,1)}, bf16[128,1024]{1,0:T(8,128)(2,1)S(1)}, bf16[128,1024]{1,0:T(8,128)(2,1)S(1)}) custom-call(s32[9]{0:T(128)S(1)} %stack.50.refs_0_, s32[16]{0:T(128)S(1)} %copy-done.5, f32[32]{0:T(128)S(1)} %copy-done.6, s32[1,8]{1,0:T(1,128)S(1)} %copy-done.7, ...), custom_call_target="tpu_custom_call" | custom-call | tf_op jit(solution)/shard_map/doc_attention/pallas_call | solution.py:280
  124.7 1.1 collective-permute-start.11
  125.8 1.9 %constant_dynamic-update-slice_fusion.3 = bf16[128,4096]{1,0:T(8,128)(2,1)} fusion(bf16[128,4096]{1,0:T(8,128)(2,1)} %get-tuple-element.9, bf16[128,2048]{1,0:T(8,128)(2,1)} %collective-permute-done.1, s32[]{:T(128)S(6)} %select_n.51), kind=kLoop, calls=%fused_computation.12 | loop fusion | bytes 1048580 | tf_op jit(solution)/shard_map/dynamic_update_slice | solution.py:469
  127.7 3.9 %collective-permute-done.9 = bf16[128,1024]{1,0:T(8,128)(2,1)S(1)} collective-permute-done((bf16[128,1024]{1,0:T(8,128)(2,1)}, bf16[128,1024]{1,0:T(8,128)(2,1)S(1)}, u32[]{:S(2)}, u32[]{:S(2)}) %collective-permute-start.9) | collective-permute-done | bytes 262176 | tf_op jit(solution)/shard_map/ppermute | solution.py:486
  132.3 0.7 constant_dynamic-update-slice_fusion.1
  133.0 4.7 %collective-permute-done.11 = bf16[128,1024]{1,0:T(8,128)(2,1)S(1)} collective-permute-done((bf16[128,1024]{1,0:T(8,128)(2,1)S(1)}, bf16[128,1024]{1,0:T(8,128)(2,1)S(1)}, u32[]{:S(2)}, u32[]{:S(2)}) %collective-permute-start.11) | collective-permute-done | bytes 262176 | tf_op jit(solution)/shard_map/ppermute | solution.py:486
  137.7 0.7 constant_dynamic-update-slice_fusion
  (44 shorter events, 4.2 us)
Async XLA Ops:
  0.6 14.5 %copy-start.3 = (bf16[256,256]{1,0:T(8,128)(2,1)S(1)}, bf16[256,256]{1,0:T(8,128)(2,1)}, u32[]{:S(2)}) copy-start(bf16[256,256]{1,0:T(8,128)(2,1)} %key_ref.1) | copy-start | bytes 393220
  0.6 14.5 %copy-start.5 = (s32[16]{0:T(128)S(1)}, s32[16]{0:T(128)}, u32[]{:S(2)}) copy-start(s32[16]{0:T(128)} %refs_1_.5) | copy-start | bytes 196
  0.7 14.5 %copy-start.2 = (bf16[256,2048]{1,0:T(8,128)(2,1)S(1)}, bf16[256,2048]{1,0:T(8,128)(2,1)}, u32[]{:S(2)}) copy-start(bf16[256,2048]{1,0:T(8,128)(2,1)} %query_ref.1) | copy-start | bytes 3145732
  0.7 38.9 %copy-start.7 = (s32[1,8]{1,0:T(1,128)S(1)}, s32[1,8]{1,0:T(1,128)}, u32[]{:S(2)}) copy-start(s32[1,8]{1,0:T(1,128)} %refs_3_.5) | copy-start | bytes 100
  0.7 54.0 %copy-start.1 = (bf16[256,2048]{1,0:T(8,128)(2,1)S(1)}, bf16[256,2048]{1,0:T(8,128)(2,1)}, u32[]{:S(2)}) copy-start(bf16[256,2048]{1,0:T(8,128)(2,1)} %refs_5_.5) | copy-start | bytes 3145732
  0.7 54.0 %copy-start.6 = (f32[32]{0:T(128)S(1)}, f32[32]{0:T(128)}, u32[]{:S(2)}) copy-start(f32[32]{0:T(128)} %refs_2_.5) | copy-start | bytes 388
  1.8 2.5 %copy-start.9 = (bf16[256,128]{1,0:T(8,128)(2,1)}, bf16[256,128]{1,0:T(8,128)(2,1)S(1)}, u32[]{:S(2)}) copy-start(bf16[256,128]{1,0:T(8,128)(2,1)S(1)} %get-tuple-element.18) | copy-start | bytes 196612
  1.8 5.7 %copy-start.10 = (bf16[256,128]{1,0:T(8,128)(2,1)}, bf16[256,128]{1,0:T(8,128)(2,1)S(1)}, u32[]{:S(2)}) copy-start(bf16[256,128]{1,0:T(8,128)(2,1)S(1)} %get-tuple-element.21) | copy-start | bytes 196612
  1.9 2.4 %collective-permute-start.3 = (bf16[256,256]{1,0:T(8,128)(2,1)S(1)}, bf16[256,256]{1,0:T(8,128)(2,1)S(1)}, u32[]{:S(2)}, u32[]{:S(2)}) collective-permute-start(bf16[256,256]{1,0:T(8,128)(2,1)S(1)} %pad_maximum_fusion.2), channel_id=1, source_target_pairs={{0,2},{2,0},{4,6},{6,4},{8,10},{10,8},{12,14},{14,12},{16,18},{18,... | collective-permute-start | bytes 393224 | tf_op jit(solution)/shard_map/ppermute | solution.py:426
  4.3 4.6 %copy-start.11 = (bf16[256,256]{1,0:T(8,128)(2,1)}, bf16[256,256]{1,0:T(8,128)(2,1)S(1)}, u32[]{:S(2)}) copy-start(bf16[256,256]{1,0:T(8,128)(2,1)S(1)} %collective-permute-done.3) | copy-start | bytes 393220
  4.4 32.6 %collective-permute-start.5 = (bf16[512,256]{1,0:T(8,128)(2,1)S(1)}, bf16[512,256]{1,0:T(8,128)(2,1)S(1)}, u32[]{:S(2)}, u32[]{:S(2)}) collective-permute-start(bf16[512,256]{1,0:T(8,128)(2,1)S(1)} %pad_maximum_fusion.refs_7_), channel_id=1, source_target_pairs={{0,8},{2,10},{4,12},{6,14},{8,16},{10,18},{12,20},{14,22},{16,24},... | collective-permute-start | bytes 786440 | tf_op jit(solution)/shard_map/ppermute | solution.py:421
  7.6 30.9 %collective-permute-start.7 = (bf16[512,256]{1,0:T(8,128)(2,1)S(1)}, bf16[512,256]{1,0:T(8,128)(2,1)S(1)}, u32[]{:S(2)}, u32[]{:S(2)}) collective-permute-start(bf16[512,256]{1,0:T(8,128)(2,1)S(1)} %pad_maximum_fusion.refs_7_), channel_id=1, source_target_pairs={{0,16},{2,18},{4,20},{6,22},{8,24},{10,26},{12,28},{14,30},{1,17},... | collective-permute-start | bytes 786440 | tf_op jit(solution)/shard_map/ppermute | solution.py:421
  9.6 5.5 %collective-permute-start = (bf16[128,512]{1,0:T(8,128)(2,1)}, bf16[128,512]{1,0:T(8,128)(2,1)}, u32[]{:S(2)}, u32[]{:S(2)}) collective-permute-start(bf16[128,512]{1,0:T(8,128)(2,1)} %pad_maximum_fusion.1), channel_id=1, source_target_pairs={{0,2},{2,4},{4,6},{6,8},{8,10},{10,12},{12,14},{14,16},{16,18},{18... | collective-permute-start | bytes 393224 | tf_op jit(solution)/shard_map/ppermute | solution.py:421
  14.7 40.0 %collective-permute-start.4 = (bf16[256,1024]{1,0:T(8,128)(2,1)}, bf16[256,1024]{1,0:T(8,128)(2,1)S(1)}, u32[]{:S(2)}, u32[]{:S(2)}) collective-permute-start(bf16[256,1024]{1,0:T(8,128)(2,1)} %constant_dynamic-slice_fusion), channel_id=1, source_target_pairs={{0,2},{2,0},{4,6},{6,4},{8,10},{10,8},{12,14},{14,12},{16,18},{18,... | collective-permute-start | bytes 1572872 | tf_op jit(solution)/shard_map/ppermute | solution.py:426
  15.1 0.9 copy-start.4
  16.0 0.7 copy-start.8
  35.7 90.1 %collective-permute-start.1 = (bf16[128,2048]{1,0:T(8,128)(2,1)}, bf16[128,2048]{1,0:T(8,128)(2,1)}, u32[]{:S(2)}, u32[]{:S(2)}) collective-permute-start(bf16[128,2048]{1,0:T(8,128)(2,1)} %get-tuple-element.10), channel_id=1, source_target_pairs={{0,1},{1,0},{2,3},{3,2},{4,5},{5,4},{6,7},{7,6},{8,9},{9,8},{10,11... | collective-permute-start | bytes 1572872 | tf_op jit(solution)/shard_map/ppermute | solution.py:468
  36.9 28.6 %collective-permute-start.6 = (bf16[512,256]{1,0:T(8,128)(2,1)S(1)}, bf16[512,256]{1,0:T(8,128)(2,1)S(1)}, u32[]{:S(2)}, u32[]{:S(2)}) collective-permute-start(bf16[512,256]{1,0:T(8,128)(2,1)S(1)} %collective-permute-done.5.refs_8_), channel_id=1, source_target_pairs={{0,4},{2,6},{4,0},{6,2},{8,12},{10,14},{12,8},{14,10},{16,20},{18,... | collective-permute-start | bytes 786440 | tf_op jit(solution)/shard_map/ppermute | solution.py:426
  39.5 38.1 %collective-permute-start.8 = (bf16[512,256]{1,0:T(8,128)(2,1)S(1)}, bf16[512,256]{1,0:T(8,128)(2,1)S(1)}, u32[]{:S(2)}, u32[]{:S(2)}) collective-permute-start(bf16[512,256]{1,0:T(8,128)(2,1)S(1)} %broadcast_select_fusion), channel_id=1, source_target_pairs={{0,4},{2,6},{4,0},{6,2},{8,12},{10,14},{12,8},{14,10},{16,20},{18,... | collective-permute-start | bytes 786440 | tf_op jit(solution)/shard_map/ppermute | solution.py:426
  39.5 15.2 %collective-permute-start.2 = (s32[1,8]{1,0:T(1,128)S(1)}, s32[1,8]{1,0:T(1,128)S(1)}, u32[]{:S(2)}, u32[]{:S(2)}) collective-permute-start(s32[1,8]{1,0:T(1,128)S(1)} %copy-done.7), channel_id=1, source_target_pairs={{0,2},{2,0},{4,6},{6,4},{8,10},{10,8},{12,14},{14,12},{16,18},{18,... | collective-permute-start | bytes 104 | tf_op jit(solution)/shard_map/ppermute | solution.py:426
  76.1 1.5 %copy-start = (f32[4,80,2048]{2,1,0:T(8,128)}, f32[4,80,2048]{2,1,0:T(8,128)S(1)}, u32[]{:S(2)}) copy-start(f32[4,80,2048]{2,1,0:T(8,128)S(1)} %doc_attention.4.refs_12_) | copy-start | bytes 7864324
  123.8 7.8 %collective-permute-start.9 = (bf16[128,1024]{1,0:T(8,128)(2,1)}, bf16[128,1024]{1,0:T(8,128)(2,1)S(1)}, u32[]{:S(2)}, u32[]{:S(2)}) collective-permute-start(bf16[128,1024]{1,0:T(8,128)(2,1)} %get-tuple-element.13), channel_id=1, source_target_pairs={{0,1},{1,0},{2,3},{3,2},{4,5},{5,4},{6,7},{7,6},{8,9},{9,8},{10,11... | collective-permute-start | bytes 786440 | tf_op jit(solution)/shard_map/ppermute | solution.py:486
  124.0 8.2 %collective-permute-start.10 = (bf16[128,1024]{1,0:T(8,128)(2,1)S(1)}, bf16[128,1024]{1,0:T(8,128)(2,1)S(1)}, u32[]{:S(2)}, u32[]{:S(2)}) collective-permute-start(bf16[128,1024]{1,0:T(8,128)(2,1)S(1)} %get-tuple-element.14), channel_id=1, source_target_pairs={{0,2},{1,3},{2,0},{3,1},{4,6},{5,7},{6,4},{7,5},{8,10},{9,11},{10,... | collective-permute-start | bytes 786440 | tf_op jit(solution)/shard_map/ppermute | solution.py:486
  124.7 13.0 %collective-permute-start.11 = (bf16[128,1024]{1,0:T(8,128)(2,1)S(1)}, bf16[128,1024]{1,0:T(8,128)(2,1)S(1)}, u32[]{:S(2)}, u32[]{:S(2)}) collective-permute-start(bf16[128,1024]{1,0:T(8,128)(2,1)S(1)} %get-tuple-element.15), channel_id=1, source_target_pairs={{0,3},{1,2},{2,1},{3,0},{4,7},{5,6},{6,5},{7,4},{8,11},{9,10},{10,... | collective-permute-start | bytes 786440 | tf_op jit(solution)/shard_map/ppermute | solution.py:486

commit v3 on v2

--- a/solution.py
+++ b/solution.py
@@ -102,7 +102,7 @@
 
 
 class DocPlan:
-    def __init__(self, first, last, grp, heads, earlier, units, rows, pieces, wide=4):
+    def __init__(self, first, last, grp, heads, earlier, units, rows, pieces, wide=8):
         self.first, self.last, self.grp, self.heads = first, last, grp, heads
         self.earlier, self.units, self.rows, self.pieces = earlier, units, rows, pieces
         self.wide = wide
@@ -366,7 +366,7 @@
 
 
 def band_call(where, starts, sinks, queries, keys, value_rows, rim, heads, rows, pieces, columns):
-    wide = 4
+    wide = 8
     steps = heads * G // wide
     size = wide * HD
     width = heads * HD
@@ -450,6 +450,7 @@
         return lax.dynamic_slice_in_dim(value, which * size, size, axis=1)
 
     away = jnp.concatenate([half(k_doc, 1 - core, width), half(v_doc, 1 - core, width)], axis=1)
+    away, mate_lists = lax.optimization_barrier((away, swapped(source_lists, 1)))
     near = swapped(away, 1)
     rim = jnp.concatenate([k_band[rows - WIN :], v_band[rows - WIN :]], axis=1)
     rim = shifted(rim, 1)
@@ -458,7 +459,6 @@
     back4 = shifted(unit, 4)
     back8 = shifted(unit, 8)
     q_later, _ = lax.optimization_barrier((q_doc, unit))
-    mate_lists = swapped(source_lists, 1)
     q_mate = swapped(half(q_later, 1 - core, mine * G * HD), 1)
     cross4 = swapped(back4, 2)
     late = swapped(jnp.where(layer == 0, unit, back8), 2)
@@ -478,8 +478,7 @@
     units = [unit, back4, cross4, back8, late]
     dists = [0, 4, 4 + flip, 8, jnp.where(layer == 0, 6, 2)]
     (state,) = doc(True, False, units[:2], dists[:2], 0, None)
-    (state,) = doc(False, False, units[2:4], dists[2:4], 0, state)
-    out_doc, *sends = doc(False, True, units, dists, 4, state)
+    out_doc, *sends = doc(False, True, units, dists, 2, state)
     size = mine * G * HD
     for mask, send in zip((1, 2, 3), sends):
         count = 2 * lax.axis_size("seq")

time: 139 us -> 115 us (0.83)
  Pallas kernels: 86.6 us -> 67.6 us
  starting transfers between devices: 27.7 us -> 24.4 us
  waiting for transfers between devices: 9.41 us -> 6.3 us
    ppermute x5, starting transfers between devices: 16.7 us -> 2.45 us  [swapped(): return lax.ppermute(value, 'seq', [(i, i ^ bit) for i in range(count)])]
    pallas_call x3 -> x2, Pallas kernels: 67.6 us -> 54 us  [doc_call(): pl.pallas_call(functools.partial(doc_body, plan), out_shape=out_shape, gr...]
    ppermute x3, starting transfers between devices: 1.98 us -> 12.8 us  [paired_program(): lax.ppermute(send, ('seq', 'kv'), [(i, i ^ mask) for i in range(count)])]
    pallas_call x1, Pallas kernels: 19 us -> 13.5 us  [band_call(): pl.pallas_call(functools.partial(band_body, heads, rows, wide, pieces), o...]
    ppermute x3, waiting for transfers between devices: 8.55 us -> 6.28 us  [paired_program(): lax.ppermute(send, ('seq', 'kv'), [(i, i ^ mask) for i in range(count)])]
    unnamed x24 -> x28, local copies, waits for them, and re-layouts: 3.09 us -> 4.33 us
  transfers between devices with their start and end apart: 12 -> 12, of which waited for: 4 -> 1; matrix products, arithmetic and copies ran while one was open for 6% -> 9% of each run, Pallas kernels for 63% -> 59%
where the time goes in v3:
time: 115 us; the launch traced here: 114 us
  Pallas kernels  67.6 us (59%)
  starting transfers between devices  24.4 us (21%)
  local copies, waits for them, and re-layouts  13.1 us (11%)
  waiting for transfers between devices  6.3 us (5%)
  other arithmetic  1.8 us (2%)
    pallas_call x2, Pallas kernels, doc_call(): pl.pallas_call(functools.partial(doc_body, plan), out_shape=out_shape, gr...  54 us
    pallas_call x1, Pallas kernels, band_call(): pl.pallas_call(functools.partial(band_body, heads, rows, wide, pieces), o...  13.5 us
    ppermute x3, starting transfers between devices, paired_program(): lax.ppermute(send, ('seq', 'kv'), [(i, i ^ mask) for i in range(count)])  12.8 us
    ppermute x3, starting transfers between devices, shifted(): lax.ppermute(value, 'seq', [(i, i + steps) for i in range(count - steps)])  7.89 us
    ppermute x3, waiting for transfers between devices, paired_program(): lax.ppermute(send, ('seq', 'kv'), [(i, i ^ mask) for i in range(count)])  6.28 us
    unnamed x28, local copies, waits for them, and re-layouts  4.33 us
    dynamic_slice x2, local copies, waits for them, and re-layouts, half(): return lax.dynamic_slice_in_dim(value, which * size, size, axis=1)  2.91 us
    ppermute x5, starting transfers between devices, swapped(): return lax.ppermute(value, 'seq', [(i, i ^ bit) for i in range(count)])  2.45 us
  transfers between devices with their start and end apart: 12, of which 1 were waited for; matrix products, arithmetic and copies ran while one was open for 9% of the time, Pallas kernels for 59%

profile of v3, /device:TPU:17, one launch (start us, length us, event | category | flops | bytes accessed | tf_op | source)
XLA Modules:
  0.0 114.0 jit_solution(14302429866437869903)
XLA Ops:
  0.7 0.7 collective-permute-start.2
  1.4 1.0 constant_dynamic-slice_fusion.1
  2.7 0.8 slice.6
  3.5 0.8 slice.7
  5.1 1.3 %collective-permute-start.7 = (bf16[512,256]{1,0:T(8,128)(2,1)S(1)}, bf16[512,256]{1,0:T(8,128)(2,1)S(1)}, u32[]{:S(2)}, u32[]{:S(2)}) collective-permute-start(bf16[512,256]{1,0:T(8,128)(2,1)S(1)} %pad_maximum_fusion.refs_7_), channel_id=1, source_target_pairs={{0,16},{2,18},{4,20},{6,22},{8,24},{10,26},{12,28},{14,30},{1,17},... | collective-permute-start | bytes 786440 | tf_op jit(solution)/shard_map/ppermute | solution.py:421
  6.4 0.7 pad_maximum_fusion.1
  7.1 3.4 %collective-permute-start = (bf16[128,512]{1,0:T(8,128)(2,1)}, bf16[128,512]{1,0:T(8,128)(2,1)}, u32[]{:S(2)}, u32[]{:S(2)}) collective-permute-start(bf16[128,512]{1,0:T(8,128)(2,1)} %pad_maximum_fusion.1), channel_id=1, source_target_pairs={{0,2},{2,4},{4,6},{6,8},{8,10},{10,12},{12,14},{14,16},{16,18},{18... | collective-permute-start | bytes 393224 | tf_op jit(solution)/shard_map/ppermute | solution.py:421
  10.5 3.2 %collective-permute-start.5 = (bf16[512,256]{1,0:T(8,128)(2,1)S(1)}, bf16[512,256]{1,0:T(8,128)(2,1)S(1)}, u32[]{:S(2)}, u32[]{:S(2)}) collective-permute-start(bf16[512,256]{1,0:T(8,128)(2,1)S(1)} %pad_maximum_fusion.refs_7_), channel_id=1, source_target_pairs={{0,8},{2,10},{4,12},{6,14},{8,16},{10,18},{12,20},{14,22},{16,24},... | collective-permute-start | bytes 786440 | tf_op jit(solution)/shard_map/ppermute | solution.py:421
  13.7 1.9 %constant_dynamic-slice_fusion = bf16[256,1024]{1,0:T(8,128)(2,1)} fusion(bf16[256,2048]{1,0:T(8,128)(2,1)} %refs_5_.3, s32[]{:T(128)S(6)} %select_n.57), kind=kLoop, calls=%fused_computation.7 | loop fusion | bytes 1048580 | tf_op jit(solution)/shard_map/dynamic_slice | solution.py:450
  15.7 0.9 copy-done.4
  17.2 13.5 %band_attention.1 = (bf16[128,4096]{1,0:T(8,128)(2,1)}, bf16[128,2048]{1,0:T(8,128)(2,1)}) custom-call(s32[4]{0:T(128)S(1)} %pad_add_fusion.where_ref, s32[16]{0:T(128)S(1)} %copy-done.5, f32[32]{0:T(128)S(1)} %copy-done.10, bf16[256,2048]{1,0:T(8,128)(2,1)S(1)} %copy-done.2, bf16[256,256]{1,0:T(8,128)(2,1)S(1)} %copy-done.3, ...), custom_call_target="tpu_custom_call" | custom-call | tf_op jit(solution)/shard_map/band_attention/pallas_call | solution.py:391
  30.8 1.2 %collective-permute-start.1 = (bf16[128,2048]{1,0:T(8,128)(2,1)}, bf16[128,2048]{1,0:T(8,128)(2,1)}, u32[]{:S(2)}, u32[]{:S(2)}) collective-permute-start(bf16[128,2048]{1,0:T(8,128)(2,1)} %get-tuple-element.12), channel_id=1, source_target_pairs={{0,1},{1,0},{2,3},{3,2},{4,5},{5,4},{6,7},{7,6},{8,9},{9,8},{10,11... | collective-permute-start | bytes 1572872 | tf_op jit(solution)/shard_map/ppermute | solution.py:468
  32.0 1.0 broadcast_select_fusion
  33.6 1.0 collective-permute-start.6
  35.4 9.3 %doc_attention.2.refs_12_ = f32[2,80,4096]{2,1,0:T(8,128)S(1)} custom-call(s32[6]{0:T(128)S(1)} %stack.43.refs_0_, s32[16]{0:T(128)S(1)} %copy-done.5, f32[32]{0:T(128)S(1)} %copy-done.6, s32[1,8]{1,0:T(1,128)S(1)} %copy-done.7, s32[1,8]{1,0:T(1,128)S(1)} %copy-done.9, bf16[256,2048]{1,0:T(8,128)(2,1)S(1)} %copy-done.1, ...), custom_call_target="tpu_custom_call" | custom-call | tf_op jit(solution)/shard_map/doc_attention/pallas_call | solution.py:280
  44.7 1.5 %copy-done = f32[2,80,4096]{2,1,0:T(8,128)} copy-done((f32[2,80,4096]{2,1,0:T(8,128)}, f32[2,80,4096]{2,1,0:T(8,128)S(1)}, u32[]{:S(2)}) %copy-start) | copy-done | bytes 2621464
  46.2 44.7 %doc_attention.3 = (bf16[128,4096]{1,0:T(8,128)(2,1)}, bf16[128,1024]{1,0:T(8,128)(2,1)}, bf16[128,1024]{1,0:T(8,128)(2,1)S(1)}, bf16[128,1024]{1,0:T(8,128)(2,1)S(1)}) custom-call(s32[9]{0:T(128)S(1)} %stack.42.refs_0_, s32[16]{0:T(128)S(1)} %copy-done.5, f32[32]{0:T(128)S(1)} %copy-done.6, s32[1,8]{1,0:T(1,128)S(1)} %copy-done.7, s32[1,8]{1,0:T(1,128)S(1)} %copy-done.9, ...), custom_call_target="tpu_custom_call" | custom-call | tf_op jit(solution)/shard_map/doc_attention/pallas_call | solution.py:280
  91.1 11.5 %collective-permute-start.10 = (bf16[128,1024]{1,0:T(8,128)(2,1)S(1)}, bf16[128,1024]{1,0:T(8,128)(2,1)S(1)}, u32[]{:S(2)}, u32[]{:S(2)}) collective-permute-start(bf16[128,1024]{1,0:T(8,128)(2,1)S(1)} %get-tuple-element.18), channel_id=1, source_target_pairs={{0,2},{1,3},{2,0},{3,1},{4,6},{5,7},{6,4},{7,5},{8,10},{9,11},{10,... | collective-permute-start | bytes 786440 | tf_op jit(solution)/shard_map/ppermute | solution.py:485
  102.6 1.1 collective-permute-start.11
  103.7 1.9 %constant_dynamic-update-slice_fusion.3 = bf16[128,4096]{1,0:T(8,128)(2,1)} fusion(bf16[128,4096]{1,0:T(8,128)(2,1)} %get-tuple-element.11, bf16[128,2048]{1,0:T(8,128)(2,1)} %collective-permute-done.1, s32[]{:T(128)S(6)} %select_n.51), kind=kLoop, calls=%fused_computation.12 | loop fusion | bytes 1048580 | tf_op jit(solution)/shard_map/dynamic_update_slice | solution.py:469
  105.6 0.7 constant_dynamic-update-slice_fusion.2
  106.3 0.7 constant_dynamic-update-slice_fusion.1
  107.1 6.3 %collective-permute-done.11 = bf16[128,1024]{1,0:T(8,128)(2,1)S(1)} collective-permute-done((bf16[128,1024]{1,0:T(8,128)(2,1)S(1)}, bf16[128,1024]{1,0:T(8,128)(2,1)S(1)}, u32[]{:S(2)}, u32[]{:S(2)}) %collective-permute-start.11) | collective-permute-done | bytes 262176 | tf_op jit(solution)/shard_map/ppermute | solution.py:485
  113.3 0.7 constant_dynamic-update-slice_fusion
  (46 shorter events, 3.2 us)
Async XLA Ops:
  0.6 15.0 %copy-start.3 = (bf16[256,256]{1,0:T(8,128)(2,1)S(1)}, bf16[256,256]{1,0:T(8,128)(2,1)}, u32[]{:S(2)}) copy-start(bf16[256,256]{1,0:T(8,128)(2,1)} %key_ref.1) | copy-start | bytes 393220
  0.6 15.0 %copy-start.5 = (s32[16]{0:T(128)S(1)}, s32[16]{0:T(128)}, u32[]{:S(2)}) copy-start(s32[16]{0:T(128)} %refs_1_.3) | copy-start | bytes 196
  0.7 15.0 %copy-start.2 = (bf16[256,2048]{1,0:T(8,128)(2,1)S(1)}, bf16[256,2048]{1,0:T(8,128)(2,1)}, u32[]{:S(2)}) copy-start(bf16[256,2048]{1,0:T(8,128)(2,1)} %query_ref.1) | copy-start | bytes 3145732
  0.7 1.8 %collective-permute-start.2 = (s32[1,8]{1,0:T(1,128)}, s32[1,8]{1,0:T(1,128)S(1)}, u32[]{:S(2)}, u32[]{:S(2)}) collective-permute-start(s32[1,8]{1,0:T(1,128)} %refs_3_.3), channel_id=1, source_target_pairs={{0,2},{2,0},{4,6},{6,4},{8,10},{10,8},{12,14},{14,12},{16,18},{18,... | collective-permute-start | bytes 104 | tf_op jit(solution)/shard_map/ppermute | solution.py:426
  1.4 33.3 %copy-start.1 = (bf16[256,2048]{1,0:T(8,128)(2,1)S(1)}, bf16[256,2048]{1,0:T(8,128)(2,1)}, u32[]{:S(2)}) copy-start(bf16[256,2048]{1,0:T(8,128)(2,1)} %refs_5_.3) | copy-start | bytes 3145732
  1.4 33.3 %copy-start.6 = (f32[32]{0:T(128)S(1)}, f32[32]{0:T(128)}, u32[]{:S(2)}) copy-start(f32[32]{0:T(128)} %refs_2_.3) | copy-start | bytes 388
  1.4 33.3 %copy-start.7 = (s32[1,8]{1,0:T(1,128)S(1)}, s32[1,8]{1,0:T(1,128)}, u32[]{:S(2)}) copy-start(s32[1,8]{1,0:T(1,128)} %refs_3_.3) | copy-start | bytes 100
  2.5 1.9 %copy-start.11 = (bf16[256,128]{1,0:T(8,128)(2,1)}, bf16[256,128]{1,0:T(8,128)(2,1)S(1)}, u32[]{:S(2)}) copy-start(bf16[256,128]{1,0:T(8,128)(2,1)S(1)} %get-tuple-element.22) | copy-start | bytes 196612
  2.5 1.9 %copy-start.12 = (bf16[256,128]{1,0:T(8,128)(2,1)}, bf16[256,128]{1,0:T(8,128)(2,1)S(1)}, u32[]{:S(2)}) copy-start(bf16[256,128]{1,0:T(8,128)(2,1)S(1)} %get-tuple-element.25) | copy-start | bytes 196612
  2.5 13.0 %copy-start.8 = (s32[1,8]{1,0:T(1,128)}, s32[1,8]{1,0:T(1,128)S(1)}, u32[]{:S(2)}) copy-start(s32[1,8]{1,0:T(1,128)S(1)} %collective-permute-done.2.refs_4_) | copy-start | bytes 100
  2.5 1.9 %collective-permute-start.3 = (bf16[256,256]{1,0:T(8,128)(2,1)S(1)}, bf16[256,256]{1,0:T(8,128)(2,1)S(1)}, u32[]{:S(2)}, u32[]{:S(2)}) collective-permute-start(bf16[256,256]{1,0:T(8,128)(2,1)S(1)} %pad_maximum_fusion.2), channel_id=1, source_target_pairs={{0,2},{2,0},{4,6},{6,4},{8,10},{10,8},{12,14},{14,12},{16,18},{18,... | collective-permute-start | bytes 393224 | tf_op jit(solution)/shard_map/ppermute | solution.py:426
  4.4 0.7 copy-start.13
  5.1 26.9 %collective-permute-start.7 = (bf16[512,256]{1,0:T(8,128)(2,1)S(1)}, bf16[512,256]{1,0:T(8,128)(2,1)S(1)}, u32[]{:S(2)}, u32[]{:S(2)}) collective-permute-start(bf16[512,256]{1,0:T(8,128)(2,1)S(1)} %pad_maximum_fusion.refs_7_), channel_id=1, source_target_pairs={{0,16},{2,18},{4,20},{6,22},{8,24},{10,26},{12,28},{14,30},{1,17},... | collective-permute-start | bytes 786440 | tf_op jit(solution)/shard_map/ppermute | solution.py:421
  7.1 8.6 %collective-permute-start = (bf16[128,512]{1,0:T(8,128)(2,1)}, bf16[128,512]{1,0:T(8,128)(2,1)}, u32[]{:S(2)}, u32[]{:S(2)}) collective-permute-start(bf16[128,512]{1,0:T(8,128)(2,1)} %pad_maximum_fusion.1), channel_id=1, source_target_pairs={{0,2},{2,4},{4,6},{6,8},{8,10},{10,12},{12,14},{14,16},{16,18},{18... | collective-permute-start | bytes 393224 | tf_op jit(solution)/shard_map/ppermute | solution.py:421
  10.5 23.1 %collective-permute-start.5 = (bf16[512,256]{1,0:T(8,128)(2,1)S(1)}, bf16[512,256]{1,0:T(8,128)(2,1)S(1)}, u32[]{:S(2)}, u32[]{:S(2)}) collective-permute-start(bf16[512,256]{1,0:T(8,128)(2,1)S(1)} %pad_maximum_fusion.refs_7_), channel_id=1, source_target_pairs={{0,8},{2,10},{4,12},{6,14},{8,16},{10,18},{12,20},{14,22},{16,24},... | collective-permute-start | bytes 786440 | tf_op jit(solution)/shard_map/ppermute | solution.py:421
  15.6 19.2 %collective-permute-start.4 = (bf16[256,1024]{1,0:T(8,128)(2,1)}, bf16[256,1024]{1,0:T(8,128)(2,1)S(1)}, u32[]{:S(2)}, u32[]{:S(2)}) collective-permute-start(bf16[256,1024]{1,0:T(8,128)(2,1)} %constant_dynamic-slice_fusion), channel_id=1, source_target_pairs={{0,2},{2,0},{4,6},{6,4},{8,10},{10,8},{12,14},{14,12},{16,18},{18,... | collective-permute-start | bytes 1572872 | tf_op jit(solution)/shard_map/ppermute | solution.py:426
  15.7 0.9 copy-start.4
  30.8 73.0 %collective-permute-start.1 = (bf16[128,2048]{1,0:T(8,128)(2,1)}, bf16[128,2048]{1,0:T(8,128)(2,1)}, u32[]{:S(2)}, u32[]{:S(2)}) collective-permute-start(bf16[128,2048]{1,0:T(8,128)(2,1)} %get-tuple-element.12), channel_id=1, source_target_pairs={{0,1},{1,0},{2,3},{3,2},{4,5},{5,4},{6,7},{7,6},{8,9},{9,8},{10,11... | collective-permute-start | bytes 1572872 | tf_op jit(solution)/shard_map/ppermute | solution.py:468
  33.0 13.1 %collective-permute-start.8 = (bf16[512,256]{1,0:T(8,128)(2,1)S(1)}, bf16[512,256]{1,0:T(8,128)(2,1)S(1)}, u32[]{:S(2)}, u32[]{:S(2)}) collective-permute-start(bf16[512,256]{1,0:T(8,128)(2,1)S(1)} %broadcast_select_fusion), channel_id=1, source_target_pairs={{0,4},{2,6},{4,0},{6,2},{8,12},{10,14},{12,8},{14,10},{16,20},{18,... | collective-permute-start | bytes 786440 | tf_op jit(solution)/shard_map/ppermute | solution.py:426
  33.6 12.6 %collective-permute-start.6 = (bf16[512,256]{1,0:T(8,128)(2,1)S(1)}, bf16[512,256]{1,0:T(8,128)(2,1)S(1)}, u32[]{:S(2)}, u32[]{:S(2)}) collective-permute-start(bf16[512,256]{1,0:T(8,128)(2,1)S(1)} %collective-permute-done.5.refs_8_), channel_id=1, source_target_pairs={{0,4},{2,6},{4,0},{6,2},{8,12},{10,14},{12,8},{14,10},{16,20},{18,... | collective-permute-start | bytes 786440 | tf_op jit(solution)/shard_map/ppermute | solution.py:426
  44.6 1.5 %copy-start = (f32[2,80,4096]{2,1,0:T(8,128)}, f32[2,80,4096]{2,1,0:T(8,128)S(1)}, u32[]{:S(2)}) copy-start(f32[2,80,4096]{2,1,0:T(8,128)S(1)} %doc_attention.2.refs_12_) | copy-start | bytes 7864324
  90.9 14.7 %collective-permute-start.9 = (bf16[128,1024]{1,0:T(8,128)(2,1)}, bf16[128,1024]{1,0:T(8,128)(2,1)S(1)}, u32[]{:S(2)}, u32[]{:S(2)}) collective-permute-start(bf16[128,1024]{1,0:T(8,128)(2,1)} %get-tuple-element.17), channel_id=1, source_target_pairs={{0,1},{1,0},{2,3},{3,2},{4,5},{5,4},{6,7},{7,6},{8,9},{9,8},{10,11... | collective-permute-start | bytes 786440 | tf_op jit(solution)/shard_map/ppermute | solution.py:485
  91.1 15.2 %collective-permute-start.10 = (bf16[128,1024]{1,0:T(8,128)(2,1)S(1)}, bf16[128,1024]{1,0:T(8,128)(2,1)S(1)}, u32[]{:S(2)}, u32[]{:S(2)}) collective-permute-start(bf16[128,1024]{1,0:T(8,128)(2,1)S(1)} %get-tuple-element.18), channel_id=1, source_target_pairs={{0,2},{1,3},{2,0},{3,1},{4,6},{5,7},{6,4},{7,5},{8,10},{9,11},{10,... | collective-permute-start | bytes 786440 | tf_op jit(solution)/shard_map/ppermute | solution.py:485
  102.6 10.7 %collective-permute-start.11 = (bf16[128,1024]{1,0:T(8,128)(2,1)S(1)}, bf16[128,1024]{1,0:T(8,128)(2,1)S(1)}, u32[]{:S(2)}, u32[]{:S(2)}) collective-permute-start(bf16[128,1024]{1,0:T(8,128)(2,1)S(1)} %get-tuple-element.19), channel_id=1, source_target_pairs={{0,3},{1,2},{2,1},{3,0},{4,7},{5,6},{6,5},{7,4},{8,11},{9,10},{10,... | collective-permute-start | bytes 786440 | tf_op jit(solution)/shard_map/ppermute | solution.py:485
  (2 other events, 1.3 us)

commit v4 on v3

--- a/solution.py
+++ b/solution.py
@@ -453,15 +453,14 @@
     away, mate_lists = lax.optimization_barrier((away, swapped(source_lists, 1)))
     near = swapped(away, 1)
     rim = jnp.concatenate([k_band[rows - WIN :], v_band[rows - WIN :]], axis=1)
-    rim = shifted(rim, 1)
+    rim_sent, rim = rim, shifted(rim, 1)
     kept = jnp.concatenate([half(k_doc, core, width), half(v_doc, core, width)], axis=1)
     unit = jnp.concatenate([kept, near], axis=0)
     back4 = shifted(unit, 4)
     back8 = shifted(unit, 8)
-    q_later, _ = lax.optimization_barrier((q_doc, unit))
+    q_later, _, _ = lax.optimization_barrier((q_doc, unit, rim_sent))
     q_mate = swapped(half(q_later, 1 - core, mine * G * HD), 1)
     cross4 = swapped(back4, 2)
-    late = swapped(jnp.where(layer == 0, unit, back8), 2)
     band_out, band_send = band_call(
         place(), doc_starts, sink_band, q_band, k_band, v_band, rim, heads, rows, True, columns
     )
@@ -475,10 +474,14 @@
             (q_doc, q_mate), units, state, columns,
         )
 
-    units = [unit, back4, cross4, back8, late]
     dists = [0, 4, 4 + flip, 8, jnp.where(layer == 0, 6, 2)]
-    (state,) = doc(True, False, units[:2], dists[:2], 0, None)
-    out_doc, *sends = doc(False, True, units, dists, 2, state)
+    units = [unit, back4]
+    (state,) = doc(True, False, units, dists[:2], 0, None)
+    state, back8 = lax.optimization_barrier((state, back8))
+    late = swapped(jnp.where(layer == 0, unit, back8), 2)
+    units += [cross4, back8, late]
+    (state,) = doc(False, False, units[2:4], dists[2:4], 0, state)
+    out_doc, *sends = doc(False, True, units, dists, 4, state)
     size = mine * G * HD
     for mask, send in zip((1, 2, 3), sends):
         count = 2 * lax.axis_size("seq")

time: 115 us -> 124 us (1.078)
  starting transfers between devices: 24.4 us -> 29.7 us
  Pallas kernels: 67.6 us -> 71 us
  waiting for transfers between devices: 6.3 us -> 8.72 us
    pallas_call x2 -> x3, Pallas kernels: 54 us -> 57.8 us  [doc_call(): pl.pallas_call(functools.partial(doc_body, plan), out_shape=out_shape, gr...]
    ppermute x3, starting transfers between devices: 12.8 us -> 15.8 us  [paired_program(): lax.ppermute(send, ('seq', 'kv'), [(i, i ^ mask) for i in range(count)])]
    ppermute x5, starting transfers between devices: 2.45 us -> 4.62 us  [swapped(): return lax.ppermute(value, 'seq', [(i, i ^ bit) for i in range(count)])]
    ppermute x3, waiting for transfers between devices: 0.01 us -> 1.72 us  [shifted(): lax.ppermute(value, 'seq', [(i, i + steps) for i in range(count - steps)])]
    unnamed x28 -> x32, local copies, waits for them, and re-layouts: 4.33 us -> 4.66 us
  transfers between devices with their start and end apart: 12 -> 12, of which waited for: 1 -> 2; matrix products, arithmetic and copies ran while one was open for 9% -> 5% of each run, Pallas kernels for 59% -> 58%
where the time goes in v4:
time: 124 us; the launch traced here: 123 us
  Pallas kernels  71 us (57%)
  starting transfers between devices  29.7 us (24%)
  local copies, waits for them, and re-layouts  12 us (10%)
  waiting for transfers between devices  8.72 us (7%)
    pallas_call x3, Pallas kernels, doc_call(): pl.pallas_call(functools.partial(doc_body, plan), out_shape=out_shape, gr...  57.8 us
    ppermute x3, starting transfers between devices, paired_program(): lax.ppermute(send, ('seq', 'kv'), [(i, i ^ mask) for i in range(count)])  15.8 us
    pallas_call x1, Pallas kernels, band_call(): pl.pallas_call(functools.partial(band_body, heads, rows, wide, pieces), o...  13.2 us
    ppermute x3, starting transfers between devices, shifted(): lax.ppermute(value, 'seq', [(i, i + steps) for i in range(count - steps)])  7.97 us
    ppermute x3, waiting for transfers between devices, paired_program(): lax.ppermute(send, ('seq', 'kv'), [(i, i ^ mask) for i in range(count)])  6.98 us
    unnamed x32, local copies, waits for them, and re-layouts  4.66 us
    ppermute x5, starting transfers between devices, swapped(): return lax.ppermute(value, 'seq', [(i, i ^ bit) for i in range(count)])  4.62 us
  transfers between devices with their start and end apart: 12, of which 2 were waited for; matrix products, arithmetic and copies ran while one was open for 5% of the time, Pallas kernels for 58%

profile of v4, /device:TPU:17, one launch (start us, length us, event | category | flops | bytes accessed | tf_op | source)
XLA Modules:
  0.0 123.2 jit_solution(8328843620121750275)
XLA Ops:
  1.4 1.0 constant_dynamic-slice_fusion.1
  2.7 0.8 slice.6
  3.6 0.8 slice.7
  5.1 1.1 constant_dynamic-slice_fusion
  6.6 3.2 %collective-permute-start.5 = (bf16[512,256]{1,0:T(8,128)(2,1)S(1)}, bf16[512,256]{1,0:T(8,128)(2,1)}, u32[]{:S(2)}, u32[]{:S(2)}) collective-permute-start(bf16[512,256]{1,0:T(8,128)(2,1)S(1)} %pad_maximum_fusion.refs_7_), channel_id=1, source_target_pairs={{0,8},{2,10},{4,12},{6,14},{8,16},{10,18},{12,20},{14,22},{16,24},... | collective-permute-start | bytes 786440 | tf_op jit(solution)/shard_map/ppermute | solution.py:421
  9.8 1.3 %collective-permute-start.7 = (bf16[512,256]{1,0:T(8,128)(2,1)S(1)}, bf16[512,256]{1,0:T(8,128)(2,1)}, u32[]{:S(2)}, u32[]{:S(2)}) collective-permute-start(bf16[512,256]{1,0:T(8,128)(2,1)S(1)} %pad_maximum_fusion.refs_7_), channel_id=1, source_target_pairs={{0,16},{2,18},{4,20},{6,22},{8,24},{10,26},{12,28},{14,30},{1,17},... | collective-permute-start | bytes 786440 | tf_op jit(solution)/shard_map/ppermute | solution.py:421
  11.1 3.5 %collective-permute-start = (bf16[128,512]{1,0:T(8,128)(2,1)S(1)}, bf16[128,512]{1,0:T(8,128)(2,1)S(1)}, u32[]{:S(2)}, u32[]{:S(2)}) collective-permute-start(bf16[128,512]{1,0:T(8,128)(2,1)S(1)} %pad_maximum_fusion.1), channel_id=1, source_target_pairs={{0,2},{2,4},{4,6},{6,8},{8,10},{10,12},{12,14},{14,16},{16,18},{18... | collective-permute-start | bytes 393224 | tf_op jit(solution)/shard_map/ppermute | solution.py:421
  14.8 1.7 %collective-permute-done.rim_ref = bf16[128,512]{1,0:T(8,128)(2,1)S(1)} collective-permute-done((bf16[128,512]{1,0:T(8,128)(2,1)S(1)}, bf16[128,512]{1,0:T(8,128)(2,1)S(1)}, u32[]{:S(2)}, u32[]{:S(2)}) %collective-permute-start) | collective-permute-done | bytes 131104 | tf_op jit(solution)/shard_map/ppermute | solution.py:421
  16.5 13.2 %band_attention.1 = (bf16[128,4096]{1,0:T(8,128)(2,1)}, bf16[128,2048]{1,0:T(8,128)(2,1)}) custom-call(s32[4]{0:T(128)S(1)} %pad_add_fusion.where_ref, s32[16]{0:T(128)S(1)} %copy-done.6, f32[32]{0:T(128)S(1)} %copy-done.9, bf16[256,2048]{1,0:T(8,128)(2,1)S(1)} %copy-done.3, bf16[256,256]{1,0:T(8,128)(2,1)S(1)} %copy-done.4, bf16[256,256]{1,0:T(8,128)(2,1)S(1)} %copy-done.5, ...), custom_call_target="tpu_custom_call" | custom-call | tf_op jit(solution)/shard_map/band_attention/pallas_call | solution.py:391
  29.7 1.2 %collective-permute-start.1 = (bf16[128,2048]{1,0:T(8,128)(2,1)}, bf16[128,2048]{1,0:T(8,128)(2,1)}, u32[]{:S(2)}, u32[]{:S(2)}) collective-permute-start(bf16[128,2048]{1,0:T(8,128)(2,1)} %get-tuple-element.14), channel_id=1, source_target_pairs={{0,1},{1,0},{2,3},{3,2},{4,5},{5,4},{6,7},{7,6},{8,9},{9,8},{10,11... | collective-permute-start | bytes 1572872 | tf_op jit(solution)/shard_map/ppermute | solution.py:467
  31.0 2.3 %collective-permute-start.6 = (bf16[512,256]{1,0:T(8,128)(2,1)}, bf16[512,256]{1,0:T(8,128)(2,1)}, u32[]{:S(2)}, u32[]{:S(2)}) collective-permute-start(bf16[512,256]{1,0:T(8,128)(2,1)} %collective-permute-done.5.refs_8_), channel_id=1, source_target_pairs={{0,4},{2,6},{4,0},{6,2},{8,12},{10,14},{12,8},{14,10},{16,20},{18,... | collective-permute-start | bytes 786440 | tf_op jit(solution)/shard_map/ppermute | solution.py:426
  33.3 1.2 copy-done.1
  34.5 9.7 %doc_attention.3.refs_9_ = f32[2,80,4096]{2,1,0:T(8,128)S(1)} custom-call(s32[6]{0:T(128)S(1)} %stack.51.refs_0_, s32[16]{0:T(128)S(1)} %copy-done.6, f32[32]{0:T(128)S(1)} %copy-done.7, s32[1,8]{1,0:T(1,128)S(1)} %copy-done.8, s32[1,8]{1,0:T(1,128)S(1)} %collective-permute-done.2.refs_4_, bf16[256,2048]{1,0:T(8,128)(2,1)S(1)} %copy-done.1, ...), custom_call_target="tpu_custom_call" | custom-call | tf_op jit(solution)/shard_map/doc_attention/pallas_call | solution.py:280
  44.2 0.8 broadcast_select_fusion
  45.0 1.0 collective-permute-start.8
  46.2 1.2 copy-done.2
  47.4 10.2 %doc_attention.4.refs_12_ = f32[2,80,4096]{2,1,0:T(8,128)S(1)} custom-call(s32[6]{0:T(128)S(1)} %stack.52.refs_0_, s32[16]{0:T(128)S(1)} %copy-done.6, f32[32]{0:T(128)S(1)} %copy-done.7, s32[1,8]{1,0:T(1,128)S(1)} %copy-done.8, s32[1,8]{1,0:T(1,128)S(1)} %collective-permute-done.2.refs_4_, ...), custom_call_target="tpu_custom_call", output_to_operand_aliasing={{}: (9, {})} | custom-call | tf_op jit(solution)/shard_map/doc_attention/pallas_call | solution.py:280
  57.6 1.5 %copy-done = f32[2,80,4096]{2,1,0:T(8,128)} copy-done((f32[2,80,4096]{2,1,0:T(8,128)}, f32[2,80,4096]{2,1,0:T(8,128)S(1)}, u32[]{:S(2)}) %copy-start) | copy-done | bytes 2621464
  59.1 37.9 %doc_attention.5 = (bf16[128,4096]{1,0:T(8,128)(2,1)}, bf16[128,1024]{1,0:T(8,128)(2,1)S(1)}, bf16[128,1024]{1,0:T(8,128)(2,1)S(1)}, bf16[128,1024]{1,0:T(8,128)(2,1)S(1)}) custom-call(s32[9]{0:T(128)S(1)} %stack.50.refs_0_, s32[16]{0:T(128)S(1)} %copy-done.6, f32[32]{0:T(128)S(1)} %copy-done.7, s32[1,8]{1,0:T(1,128)S(1)} %copy-done.8, ...), custom_call_target="tpu_custom_call" | custom-call | tf_op jit(solution)/shard_map/doc_attention/pallas_call | solution.py:280
  97.3 14.5 %collective-permute-start.10 = (bf16[128,1024]{1,0:T(8,128)(2,1)S(1)}, bf16[128,1024]{1,0:T(8,128)(2,1)S(1)}, u32[]{:S(2)}, u32[]{:S(2)}) collective-permute-start(bf16[128,1024]{1,0:T(8,128)(2,1)S(1)} %get-tuple-element.22), channel_id=1, source_target_pairs={{0,2},{1,3},{2,0},{3,1},{4,6},{5,7},{6,4},{7,5},{8,10},{9,11},{10,... | collective-permute-start | bytes 786440 | tf_op jit(solution)/shard_map/ppermute | solution.py:488
  111.7 1.1 collective-permute-start.11
  112.9 1.1 constant_dynamic-update-slice_fusion.3
  114.0 0.8 constant_dynamic-update-slice_fusion.2
  115.5 7.0 %collective-permute-done.11 = bf16[128,1024]{1,0:T(8,128)(2,1)S(1)} collective-permute-done((bf16[128,1024]{1,0:T(8,128)(2,1)S(1)}, bf16[128,1024]{1,0:T(8,128)(2,1)S(1)}, u32[]{:S(2)}, u32[]{:S(2)}) %collective-permute-start.11) | collective-permute-done | bytes 262176 | tf_op jit(solution)/shard_map/ppermute | solution.py:488
  (52 shorter events, 4.2 us)
Async XLA Ops:
  0.6 32.6 %copy-start.8 = (s32[1,8]{1,0:T(1,128)S(1)}, s32[1,8]{1,0:T(1,128)}, u32[]{:S(2)}) copy-start(s32[1,8]{1,0:T(1,128)} %refs_3_.5) | copy-start | bytes 100
  0.6 15.9 %copy-start.4 = (bf16[256,256]{1,0:T(8,128)(2,1)S(1)}, bf16[256,256]{1,0:T(8,128)(2,1)}, u32[]{:S(2)}) copy-start(bf16[256,256]{1,0:T(8,128)(2,1)} %key_ref.1) | copy-start | bytes 393220
  0.7 15.9 %copy-start.5 = (bf16[256,256]{1,0:T(8,128)(2,1)S(1)}, bf16[256,256]{1,0:T(8,128)(2,1)}, u32[]{:S(2)}) copy-start(bf16[256,256]{1,0:T(8,128)(2,1)} %value_ref.1) | copy-start | bytes 393220
  0.7 15.8 %copy-start.6 = (s32[16]{0:T(128)S(1)}, s32[16]{0:T(128)}, u32[]{:S(2)}) copy-start(s32[16]{0:T(128)} %refs_1_.5) | copy-start | bytes 196
  0.7 15.8 %copy-start.3 = (bf16[256,2048]{1,0:T(8,128)(2,1)S(1)}, bf16[256,2048]{1,0:T(8,128)(2,1)}, u32[]{:S(2)}) copy-start(bf16[256,2048]{1,0:T(8,128)(2,1)} %query_ref.1) | copy-start | bytes 3145732
  0.7 15.8 %copy-start.9 = (f32[32]{0:T(128)S(1)}, f32[32]{0:T(128)}, u32[]{:S(2)}) copy-start(f32[32]{0:T(128)} %sink_ref.1) | copy-start | bytes 388
  0.7 32.6 %copy-start.7 = (f32[32]{0:T(128)S(1)}, f32[32]{0:T(128)}, u32[]{:S(2)}) copy-start(f32[32]{0:T(128)} %refs_2_.5) | copy-start | bytes 388
  0.7 1.7 %collective-permute-start.2 = (s32[1,8]{1,0:T(1,128)}, s32[1,8]{1,0:T(1,128)S(1)}, u32[]{:S(2)}, u32[]{:S(2)}) collective-permute-start(s32[1,8]{1,0:T(1,128)} %refs_3_.5), channel_id=1, source_target_pairs={{0,2},{2,0},{4,6},{6,4},{8,10},{10,8},{12,14},{14,12},{16,18},{18,... | collective-permute-start | bytes 104 | tf_op jit(solution)/shard_map/ppermute | solution.py:426
  2.4 7.4 %copy-start.10 = (bf16[256,128]{1,0:T(8,128)(2,1)}, bf16[256,128]{1,0:T(8,128)(2,1)S(1)}, u32[]{:S(2)}) copy-start(bf16[256,128]{1,0:T(8,128)(2,1)S(1)} %get-tuple-element.29) | copy-start | bytes 196612
  2.4 2.0 %collective-permute-start.3 = (bf16[256,256]{1,0:T(8,128)(2,1)S(1)}, bf16[256,256]{1,0:T(8,128)(2,1)S(1)}, u32[]{:S(2)}, u32[]{:S(2)}) collective-permute-start(bf16[256,256]{1,0:T(8,128)(2,1)S(1)} %pad_maximum_fusion.2), channel_id=1, source_target_pairs={{0,2},{2,0},{4,6},{6,4},{8,10},{10,8},{12,14},{14,12},{16,18},{18,... | collective-permute-start | bytes 393224 | tf_op jit(solution)/shard_map/ppermute | solution.py:426
  6.2 27.1 %collective-permute-start.4 = (bf16[256,1024]{1,0:T(8,128)(2,1)S(1)}, bf16[256,1024]{1,0:T(8,128)(2,1)S(1)}, u32[]{:S(2)}, u32[]{:S(2)}) collective-permute-start(bf16[256,1024]{1,0:T(8,128)(2,1)S(1)} %constant_dynamic-slice_fusion), channel_id=1, source_target_pairs={{0,2},{2,0},{4,6},{6,4},{8,10},{10,8},{12,14},{14,12},{16,18},{18,... | collective-permute-start | bytes 1572872 | tf_op jit(solution)/shard_map/ppermute | solution.py:426
  6.6 24.4 %collective-permute-start.5 = (bf16[512,256]{1,0:T(8,128)(2,1)S(1)}, bf16[512,256]{1,0:T(8,128)(2,1)}, u32[]{:S(2)}, u32[]{:S(2)}) collective-permute-start(bf16[512,256]{1,0:T(8,128)(2,1)S(1)} %pad_maximum_fusion.refs_7_), channel_id=1, source_target_pairs={{0,8},{2,10},{4,12},{6,14},{8,16},{10,18},{12,20},{14,22},{16,24},... | collective-permute-start | bytes 786440 | tf_op jit(solution)/shard_map/ppermute | solution.py:421
  9.8 34.4 %collective-permute-start.7 = (bf16[512,256]{1,0:T(8,128)(2,1)S(1)}, bf16[512,256]{1,0:T(8,128)(2,1)}, u32[]{:S(2)}, u32[]{:S(2)}) collective-permute-start(bf16[512,256]{1,0:T(8,128)(2,1)S(1)} %pad_maximum_fusion.refs_7_), channel_id=1, source_target_pairs={{0,16},{2,18},{4,20},{6,22},{8,24},{10,26},{12,28},{14,30},{1,17},... | collective-permute-start | bytes 786440 | tf_op jit(solution)/shard_map/ppermute | solution.py:421
  11.1 5.4 %collective-permute-start = (bf16[128,512]{1,0:T(8,128)(2,1)S(1)}, bf16[128,512]{1,0:T(8,128)(2,1)S(1)}, u32[]{:S(2)}, u32[]{:S(2)}) collective-permute-start(bf16[128,512]{1,0:T(8,128)(2,1)S(1)} %pad_maximum_fusion.1), channel_id=1, source_target_pairs={{0,2},{2,4},{4,6},{6,8},{8,10},{10,12},{12,14},{14,16},{16,18},{18... | collective-permute-start | bytes 393224 | tf_op jit(solution)/shard_map/ppermute | solution.py:421
  16.5 27.7 %copy-start.11 = (bf16[256,128]{1,0:T(8,128)(2,1)S(1)}, bf16[256,128]{1,0:T(8,128)(2,1)}, u32[]{:S(2)}) copy-start(bf16[256,128]{1,0:T(8,128)(2,1)} %copy-done.10) | copy-start | bytes 196612
  16.5 27.7 %copy-start.13 = (bf16[256,256]{1,0:T(8,128)(2,1)S(1)}, bf16[256,256]{1,0:T(8,128)(2,1)}, u32[]{:S(2)}) copy-start(bf16[256,256]{1,0:T(8,128)(2,1)} %copy-done.12) | copy-start | bytes 393220
  29.7 83.1 %collective-permute-start.1 = (bf16[128,2048]{1,0:T(8,128)(2,1)}, bf16[128,2048]{1,0:T(8,128)(2,1)}, u32[]{:S(2)}, u32[]{:S(2)}) collective-permute-start(bf16[128,2048]{1,0:T(8,128)(2,1)} %get-tuple-element.14), channel_id=1, source_target_pairs={{0,1},{1,0},{2,3},{3,2},{4,5},{5,4},{6,7},{7,6},{8,9},{9,8},{10,11... | collective-permute-start | bytes 1572872 | tf_op jit(solution)/shard_map/ppermute | solution.py:467
  31.0 15.2 %collective-permute-start.6 = (bf16[512,256]{1,0:T(8,128)(2,1)}, bf16[512,256]{1,0:T(8,128)(2,1)}, u32[]{:S(2)}, u32[]{:S(2)}) collective-permute-start(bf16[512,256]{1,0:T(8,128)(2,1)} %collective-permute-done.5.refs_8_), channel_id=1, source_target_pairs={{0,4},{2,6},{4,0},{6,2},{8,12},{10,14},{12,8},{14,10},{16,20},{18,... | collective-permute-start | bytes 786440 | tf_op jit(solution)/shard_map/ppermute | solution.py:426
  45.0 14.1 %collective-permute-start.8 = (bf16[512,256]{1,0:T(8,128)(2,1)}, bf16[512,256]{1,0:T(8,128)(2,1)}, u32[]{:S(2)}, u32[]{:S(2)}) collective-permute-start(bf16[512,256]{1,0:T(8,128)(2,1)} %broadcast_select_fusion), channel_id=1, source_target_pairs={{0,4},{2,6},{4,0},{6,2},{8,12},{10,14},{12,8},{14,10},{16,20},{18,... | collective-permute-start | bytes 786440 | tf_op jit(solution)/shard_map/ppermute | solution.py:426
  59.1 53.8 %copy-start.14 = (bf16[128,4096]{1,0:T(8,128)(2,1)S(1)}, bf16[128,4096]{1,0:T(8,128)(2,1)}, u32[]{:S(2)}) copy-start(bf16[128,4096]{1,0:T(8,128)(2,1)} %get-tuple-element.13) | copy-start | bytes 3145732
  97.0 16.9 %collective-permute-start.9 = (bf16[128,1024]{1,0:T(8,128)(2,1)S(1)}, bf16[128,1024]{1,0:T(8,128)(2,1)S(1)}, u32[]{:S(2)}, u32[]{:S(2)}) collective-permute-start(bf16[128,1024]{1,0:T(8,128)(2,1)S(1)} %get-tuple-element.21), channel_id=1, source_target_pairs={{0,1},{1,0},{2,3},{3,2},{4,5},{5,4},{6,7},{7,6},{8,9},{9,8},{10,11... | collective-permute-start | bytes 786440 | tf_op jit(solution)/shard_map/ppermute | solution.py:488
  97.3 17.5 %collective-permute-start.10 = (bf16[128,1024]{1,0:T(8,128)(2,1)S(1)}, bf16[128,1024]{1,0:T(8,128)(2,1)S(1)}, u32[]{:S(2)}, u32[]{:S(2)}) collective-permute-start(bf16[128,1024]{1,0:T(8,128)(2,1)S(1)} %get-tuple-element.22), channel_id=1, source_target_pairs={{0,2},{1,3},{2,0},{3,1},{4,6},{5,7},{6,4},{7,5},{8,10},{9,11},{10,... | collective-permute-start | bytes 786440 | tf_op jit(solution)/shard_map/ppermute | solution.py:488
  111.7 10.7 %collective-permute-start.11 = (bf16[128,1024]{1,0:T(8,128)(2,1)S(1)}, bf16[128,1024]{1,0:T(8,128)(2,1)S(1)}, u32[]{:S(2)}, u32[]{:S(2)}) collective-permute-start(bf16[128,1024]{1,0:T(8,128)(2,1)S(1)} %get-tuple-element.23), channel_id=1, source_target_pairs={{0,3},{1,2},{2,1},{3,0},{4,7},{5,6},{6,5},{7,4},{8,11},{9,10},{10,... | collective-permute-start | bytes 786440 | tf_op jit(solution)/shard_map/ppermute | solution.py:488
  113.9 9.2 %copy-start.15 = (bf16[128,4096]{1,0:T(8,128)(2,1)}, bf16[128,4096]{1,0:T(8,128)(2,1)S(1)}, u32[]{:S(2)}) copy-start(bf16[128,4096]{1,0:T(8,128)(2,1)S(1)} %constant_dynamic-update-slice_fusion.3) | copy-start | bytes 3145732
  (4 other events, 4.6 us)

commit v5 on v4

--- a/solution.py
+++ b/solution.py
@@ -453,12 +453,13 @@
     away, mate_lists = lax.optimization_barrier((away, swapped(source_lists, 1)))
     near = swapped(away, 1)
     rim = jnp.concatenate([k_band[rows - WIN :], v_band[rows - WIN :]], axis=1)
-    rim_sent, rim = rim, shifted(rim, 1)
+    rim = shifted(rim, 1)
     kept = jnp.concatenate([half(k_doc, core, width), half(v_doc, core, width)], axis=1)
     unit = jnp.concatenate([kept, near], axis=0)
+    unit, rim = lax.optimization_barrier((unit, rim))
     back4 = shifted(unit, 4)
     back8 = shifted(unit, 8)
-    q_later, _, _ = lax.optimization_barrier((q_doc, unit, rim_sent))
+    q_later, _ = lax.optimization_barrier((q_doc, unit))
     q_mate = swapped(half(q_later, 1 - core, mine * G * HD), 1)
     cross4 = swapped(back4, 2)
     band_out, band_send = band_call(

time: 124 us -> 117 us (0.944)
  the two profiles are of different devices: /device:TPU:17 before, /device:TPU:1 now
where the time goes in v5:
time: 117 us; the launch traced here: 116 us
  Pallas kernels  71 us (61%)
  starting transfers between devices  22 us (19%)
  local copies, waits for them, and re-layouts  11.3 us (10%)
  waiting for transfers between devices  10.1 us (9%)
    pallas_call x3, Pallas kernels, doc_call(): pl.pallas_call(functools.partial(doc_body, plan), out_shape=out_shape, gr...  57.8 us
    ppermute x3, starting transfers between devices, shifted(): lax.ppermute(value, 'seq', [(i, i + steps) for i in range(count - steps)])  14.9 us
    pallas_call x1, Pallas kernels, band_call(): pl.pallas_call(functools.partial(band_body, heads, rows, wide, pieces), o...  13.2 us
    ppermute x3, waiting for transfers between devices, paired_program(): lax.ppermute(send, ('seq', 'kv'), [(i, i ^ mask) for i in range(count)])  8.11 us
    unnamed x24, local copies, waits for them, and re-layouts  3.98 us
    ppermute x3, starting transfers between devices, paired_program(): lax.ppermute(send, ('seq', 'kv'), [(i, i ^ mask) for i in range(count)])  3 us
    ppermute x5, starting transfers between devices, swapped(): return lax.ppermute(value, 'seq', [(i, i ^ bit) for i in range(count)])  2.92 us
  transfers between devices with their start and end apart: 12, of which 4 were waited for; matrix products, arithmetic and copies ran while one was open for 6% of the time, Pallas kernels for 61%

profile of v5, /device:TPU:1, one launch (start us, length us, event | category | flops | bytes accessed | tf_op | source)
XLA Modules:
  0.0 116.1 jit_solution(6392655475685051073)
XLA Ops:
  0.8 1.1 constant_dynamic-slice_fusion.3
  2.3 0.8 slice.6
  3.2 0.8 slice.7
  4.0 4.5 %collective-permute-start.2 = (bf16[128,512]{1,0:T(8,128)(2,1)S(1)}, bf16[128,512]{1,0:T(8,128)(2,1)S(1)}, u32[]{:S(2)}, u32[]{:S(2)}) collective-permute-start(bf16[128,512]{1,0:T(8,128)(2,1)S(1)} %pad_maximum_fusion.2), channel_id=1, source_target_pairs={{0,2},{2,4},{4,6},{6,8},{8,10},{10,12},{12,14},{14,16},{16,18},{18... | collective-permute-start | bytes 393224 | tf_op jit(solution)/shard_map/ppermute | solution.py:421
  8.6 1.9 %collective-permute-done.2.rim_ref = bf16[128,512]{1,0:T(8,128)(2,1)S(1)} collective-permute-done((bf16[128,512]{1,0:T(8,128)(2,1)S(1)}, bf16[128,512]{1,0:T(8,128)(2,1)S(1)}, u32[]{:S(2)}, u32[]{:S(2)}) %collective-permute-start.2) | collective-permute-done | bytes 131104 | tf_op jit(solution)/shard_map/ppermute | solution.py:421
  10.5 1.1 constant_dynamic-slice_fusion
  11.6 6.1 %collective-permute-start.5 = (bf16[512,256]{1,0:T(8,128)(2,1)S(1)}, bf16[512,256]{1,0:T(8,128)(2,1)}, u32[]{:S(2)}, u32[]{:S(2)}) collective-permute-start(bf16[512,256]{1,0:T(8,128)(2,1)S(1)} %pad_maximum_fusion.refs_7_), channel_id=1, source_target_pairs={{0,8},{2,10},{4,12},{6,14},{8,16},{10,18},{12,20},{14,22},{16,24},... | collective-permute-start | bytes 786440 | tf_op jit(solution)/shard_map/ppermute | solution.py:421
  17.8 4.2 %collective-permute-start.7 = (bf16[512,256]{1,0:T(8,128)(2,1)S(1)}, bf16[512,256]{1,0:T(8,128)(2,1)}, u32[]{:S(2)}, u32[]{:S(2)}) collective-permute-start(bf16[512,256]{1,0:T(8,128)(2,1)S(1)} %pad_maximum_fusion.refs_7_), channel_id=1, source_target_pairs={{0,16},{2,18},{4,20},{6,22},{8,24},{10,26},{12,28},{14,30},{1,17},... | collective-permute-start | bytes 786440 | tf_op jit(solution)/shard_map/ppermute | solution.py:421
  22.2 13.2 %band_attention.1 = (bf16[128,4096]{1,0:T(8,128)(2,1)}, bf16[128,2048]{1,0:T(8,128)(2,1)}) custom-call(s32[4]{0:T(128)S(1)} %pad_add_fusion.where_ref, s32[16]{0:T(128)S(1)} %copy-done.6, f32[32]{0:T(128)S(1)} %copy-done.9, bf16[256,2048]{1,0:T(8,128)(2,1)S(1)} %copy-done.3, bf16[256,256]{1,0:T(8,128)(2,1)S(1)} %copy-done.4, bf16[256,256]{1,0:T(8,128)(2,1)S(1)} %copy-done.5, ...), custom_call_target="tpu_custom_call" | custom-call | tf_op jit(solution)/shard_map/band_attention/pallas_call | solution.py:391
  35.4 1.2 %collective-permute-start.3 = (bf16[128,2048]{1,0:T(8,128)(2,1)}, bf16[128,2048]{1,0:T(8,128)(2,1)}, u32[]{:S(2)}, u32[]{:S(2)}) collective-permute-start(bf16[128,2048]{1,0:T(8,128)(2,1)} %get-tuple-element.18), channel_id=1, source_target_pairs={{0,1},{1,0},{2,3},{3,2},{4,5},{5,4},{6,7},{7,6},{8,9},{9,8},{10,11... | collective-permute-start | bytes 1572872 | tf_op jit(solution)/shard_map/ppermute | solution.py:468
  36.9 1.2 %copy-done.1 = bf16[256,2048]{1,0:T(8,128)(2,1)S(1)} copy-done((bf16[256,2048]{1,0:T(8,128)(2,1)S(1)}, bf16[256,2048]{1,0:T(8,128)(2,1)}, u32[]{:S(2)}) %copy-start.1) | copy-done | bytes 1048600
  38.2 9.7 %doc_attention.3.refs_9_ = f32[2,80,4096]{2,1,0:T(8,128)S(1)} custom-call(s32[6]{0:T(128)S(1)} %stack.51.refs_0_, s32[16]{0:T(128)S(1)} %copy-done.6, f32[32]{0:T(128)S(1)} %copy-done.7, s32[1,8]{1,0:T(1,128)S(1)} %copy-done.8, s32[1,8]{1,0:T(1,128)S(1)} %collective-permute-done.refs_4_, bf16[256,2048]{1,0:T(8,128)(2,1)S(1)} %copy-done.1, ...), custom_call_target="tpu_custom_call" | custom-call | tf_op jit(solution)/shard_map/doc_attention/pallas_call | solution.py:280
  47.9 0.7 broadcast_select_fusion
  48.6 2.1 %collective-permute-start.8 = (bf16[512,256]{1,0:T(8,128)(2,1)}, bf16[512,256]{1,0:T(8,128)(2,1)}, u32[]{:S(2)}, u32[]{:S(2)}) collective-permute-start(bf16[512,256]{1,0:T(8,128)(2,1)} %broadcast_select_fusion), channel_id=1, source_target_pairs={{0,4},{2,6},{4,0},{6,2},{8,12},{10,14},{12,8},{14,10},{16,20},{18,... | collective-permute-start | bytes 786440 | tf_op jit(solution)/shard_map/ppermute | solution.py:426
  50.9 1.2 %copy-done.2 = bf16[256,2048]{1,0:T(8,128)(2,1)S(1)} copy-done((bf16[256,2048]{1,0:T(8,128)(2,1)S(1)}, bf16[256,2048]{1,0:T(8,128)(2,1)}, u32[]{:S(2)}) %copy-start.2) | copy-done | bytes 1048600
  52.1 10.2 %doc_attention.4.refs_12_ = f32[2,80,4096]{2,1,0:T(8,128)S(1)} custom-call(s32[6]{0:T(128)S(1)} %stack.52.refs_0_, s32[16]{0:T(128)S(1)} %copy-done.6, f32[32]{0:T(128)S(1)} %copy-done.7, s32[1,8]{1,0:T(1,128)S(1)} %copy-done.8, s32[1,8]{1,0:T(1,128)S(1)} %collective-permute-done.refs_4_, ...), custom_call_target="tpu_custom_call", output_to_operand_aliasing={{}: (9, {})} | custom-call | tf_op jit(solution)/shard_map/doc_attention/pallas_call | solution.py:280
  62.3 1.5 %copy-done = f32[2,80,4096]{2,1,0:T(8,128)} copy-done((f32[2,80,4096]{2,1,0:T(8,128)}, f32[2,80,4096]{2,1,0:T(8,128)S(1)}, u32[]{:S(2)}) %copy-start) | copy-done | bytes 2621464
  63.8 37.9 %doc_attention.5 = (bf16[128,4096]{1,0:T(8,128)(2,1)}, bf16[128,1024]{1,0:T(8,128)(2,1)S(1)}, bf16[128,1024]{1,0:T(8,128)(2,1)S(1)}, bf16[128,1024]{1,0:T(8,128)(2,1)S(1)}) custom-call(s32[9]{0:T(128)S(1)} %stack.50.refs_0_, s32[16]{0:T(128)S(1)} %copy-done.6, f32[32]{0:T(128)S(1)} %copy-done.7, s32[1,8]{1,0:T(1,128)S(1)} %copy-done.8, ...), custom_call_target="tpu_custom_call" | custom-call | tf_op jit(solution)/shard_map/doc_attention/pallas_call | solution.py:280
  102.0 1.6 %collective-permute-start.10 = (bf16[128,1024]{1,0:T(8,128)(2,1)S(1)}, bf16[128,1024]{1,0:T(8,128)(2,1)S(1)}, u32[]{:S(2)}, u32[]{:S(2)}) collective-permute-start(bf16[128,1024]{1,0:T(8,128)(2,1)S(1)} %get-tuple-element.26), channel_id=1, source_target_pairs={{0,2},{1,3},{2,0},{3,1},{4,6},{5,7},{6,4},{7,5},{8,10},{9,11},{10,... | collective-permute-start | bytes 786440 | tf_op jit(solution)/shard_map/ppermute | solution.py:489
  103.6 1.1 collective-permute-start.11
  104.7 1.1 constant_dynamic-update-slice_fusion.3
  105.8 2.3 %collective-permute-done.9 = bf16[128,1024]{1,0:T(8,128)(2,1)S(1)} collective-permute-done((bf16[128,1024]{1,0:T(8,128)(2,1)S(1)}, bf16[128,1024]{1,0:T(8,128)(2,1)S(1)}, u32[]{:S(2)}, u32[]{:S(2)}) %collective-permute-start.9) | collective-permute-done | bytes 262176 | tf_op jit(solution)/shard_map/ppermute | solution.py:489
  108.9 0.7 constant_dynamic-update-slice_fusion.1
  109.6 5.8 %collective-permute-done.11 = bf16[128,1024]{1,0:T(8,128)(2,1)S(1)} collective-permute-done((bf16[128,1024]{1,0:T(8,128)(2,1)S(1)}, bf16[128,1024]{1,0:T(8,128)(2,1)S(1)}, u32[]{:S(2)}, u32[]{:S(2)}) %collective-permute-start.11) | collective-permute-done | bytes 262176 | tf_op jit(solution)/shard_map/ppermute | solution.py:489
  (44 shorter events, 3.0 us)
Async XLA Ops:
  0.6 36.3 %copy-start.8 = (s32[1,8]{1,0:T(1,128)S(1)}, s32[1,8]{1,0:T(1,128)}, u32[]{:S(2)}) copy-start(s32[1,8]{1,0:T(1,128)} %refs_3_.5) | copy-start | bytes 100
  0.6 21.5 %copy-start.4 = (bf16[256,256]{1,0:T(8,128)(2,1)S(1)}, bf16[256,256]{1,0:T(8,128)(2,1)}, u32[]{:S(2)}) copy-start(bf16[256,256]{1,0:T(8,128)(2,1)} %key_ref.1) | copy-start | bytes 393220
  0.7 21.5 %copy-start.5 = (bf16[256,256]{1,0:T(8,128)(2,1)S(1)}, bf16[256,256]{1,0:T(8,128)(2,1)}, u32[]{:S(2)}) copy-start(bf16[256,256]{1,0:T(8,128)(2,1)} %value_ref.1) | copy-start | bytes 393220
  0.7 21.5 %copy-start.6 = (s32[16]{0:T(128)S(1)}, s32[16]{0:T(128)}, u32[]{:S(2)}) copy-start(s32[16]{0:T(128)} %refs_1_.5) | copy-start | bytes 196
  0.7 21.5 %copy-start.3 = (bf16[256,2048]{1,0:T(8,128)(2,1)S(1)}, bf16[256,2048]{1,0:T(8,128)(2,1)}, u32[]{:S(2)}) copy-start(bf16[256,2048]{1,0:T(8,128)(2,1)} %query_ref.1) | copy-start | bytes 3145732
  0.7 21.5 %copy-start.9 = (f32[32]{0:T(128)S(1)}, f32[32]{0:T(128)}, u32[]{:S(2)}) copy-start(f32[32]{0:T(128)} %sink_ref.1) | copy-start | bytes 388
  0.7 36.2 %copy-start.7 = (f32[32]{0:T(128)S(1)}, f32[32]{0:T(128)}, u32[]{:S(2)}) copy-start(f32[32]{0:T(128)} %refs_2_.5) | copy-start | bytes 388
  0.7 1.3 %collective-permute-start = (s32[1,8]{1,0:T(1,128)}, s32[1,8]{1,0:T(1,128)S(1)}, u32[]{:S(2)}, u32[]{:S(2)}) collective-permute-start(s32[1,8]{1,0:T(1,128)} %refs_3_.5), channel_id=1, source_target_pairs={{0,2},{2,0},{4,6},{6,4},{8,10},{10,8},{12,14},{14,12},{16,18},{18,... | collective-permute-start | bytes 104 | tf_op jit(solution)/shard_map/ppermute | solution.py:426
  2.0 6.5 %collective-permute-start.1 = (bf16[256,256]{1,0:T(8,128)(2,1)S(1)}, bf16[256,256]{1,0:T(8,128)(2,1)S(1)}, u32[]{:S(2)}, u32[]{:S(2)}) collective-permute-start(bf16[256,256]{1,0:T(8,128)(2,1)S(1)} %pad_maximum_fusion.1), channel_id=1, source_target_pairs={{0,2},{2,0},{4,6},{6,4},{8,10},{10,8},{12,14},{14,12},{16,18},{18,... | collective-permute-start | bytes 393224 | tf_op jit(solution)/shard_map/ppermute | solution.py:426
  4.0 6.4 %collective-permute-start.2 = (bf16[128,512]{1,0:T(8,128)(2,1)S(1)}, bf16[128,512]{1,0:T(8,128)(2,1)S(1)}, u32[]{:S(2)}, u32[]{:S(2)}) collective-permute-start(bf16[128,512]{1,0:T(8,128)(2,1)S(1)} %pad_maximum_fusion.2), channel_id=1, source_target_pairs={{0,2},{2,4},{4,6},{6,8},{8,10},{10,12},{12,14},{14,16},{16,18},{18... | collective-permute-start | bytes 393224 | tf_op jit(solution)/shard_map/ppermute | solution.py:421
  11.6 25.4 %collective-permute-start.4 = (bf16[256,1024]{1,0:T(8,128)(2,1)S(1)}, bf16[256,1024]{1,0:T(8,128)(2,1)S(1)}, u32[]{:S(2)}, u32[]{:S(2)}) collective-permute-start(bf16[256,1024]{1,0:T(8,128)(2,1)S(1)} %constant_dynamic-slice_fusion), channel_id=1, source_target_pairs={{0,2},{2,0},{4,6},{6,4},{8,10},{10,8},{12,14},{14,12},{16,18},{18,... | collective-permute-start | bytes 1572872 | tf_op jit(solution)/shard_map/ppermute | solution.py:426
  11.6 25.0 %collective-permute-start.5 = (bf16[512,256]{1,0:T(8,128)(2,1)S(1)}, bf16[512,256]{1,0:T(8,128)(2,1)}, u32[]{:S(2)}, u32[]{:S(2)}) collective-permute-start(bf16[512,256]{1,0:T(8,128)(2,1)S(1)} %pad_maximum_fusion.refs_7_), channel_id=1, source_target_pairs={{0,8},{2,10},{4,12},{6,14},{8,16},{10,18},{12,20},{14,22},{16,24},... | collective-permute-start | bytes 786440 | tf_op jit(solution)/shard_map/ppermute | solution.py:421
  17.8 30.1 %collective-permute-start.7 = (bf16[512,256]{1,0:T(8,128)(2,1)S(1)}, bf16[512,256]{1,0:T(8,128)(2,1)}, u32[]{:S(2)}, u32[]{:S(2)}) collective-permute-start(bf16[512,256]{1,0:T(8,128)(2,1)S(1)} %pad_maximum_fusion.refs_7_), channel_id=1, source_target_pairs={{0,16},{2,18},{4,20},{6,22},{8,24},{10,26},{12,28},{14,30},{1,17},... | collective-permute-start | bytes 786440 | tf_op jit(solution)/shard_map/ppermute | solution.py:421
  35.4 69.4 %collective-permute-start.3 = (bf16[128,2048]{1,0:T(8,128)(2,1)}, bf16[128,2048]{1,0:T(8,128)(2,1)}, u32[]{:S(2)}, u32[]{:S(2)}) collective-permute-start(bf16[128,2048]{1,0:T(8,128)(2,1)} %get-tuple-element.18), channel_id=1, source_target_pairs={{0,1},{1,0},{2,3},{3,2},{4,5},{5,4},{6,7},{7,6},{8,9},{9,8},{10,11... | collective-permute-start | bytes 1572872 | tf_op jit(solution)/shard_map/ppermute | solution.py:468
  36.6 14.3 %collective-permute-start.6 = (bf16[512,256]{1,0:T(8,128)(2,1)}, bf16[512,256]{1,0:T(8,128)(2,1)}, u32[]{:S(2)}, u32[]{:S(2)}) collective-permute-start(bf16[512,256]{1,0:T(8,128)(2,1)} %collective-permute-done.5.refs_8_), channel_id=1, source_target_pairs={{0,4},{2,6},{4,0},{6,2},{8,12},{10,14},{12,8},{14,10},{16,20},{18,... | collective-permute-start | bytes 786440 | tf_op jit(solution)/shard_map/ppermute | solution.py:426
  36.9 1.2 %copy-start.1 = (bf16[256,2048]{1,0:T(8,128)(2,1)S(1)}, bf16[256,2048]{1,0:T(8,128)(2,1)}, u32[]{:S(2)}) copy-start(bf16[256,2048]{1,0:T(8,128)(2,1)} %refs_5_.5) | copy-start | bytes 3145732
  48.6 15.2 %collective-permute-start.8 = (bf16[512,256]{1,0:T(8,128)(2,1)}, bf16[512,256]{1,0:T(8,128)(2,1)}, u32[]{:S(2)}, u32[]{:S(2)}) collective-permute-start(bf16[512,256]{1,0:T(8,128)(2,1)} %broadcast_select_fusion), channel_id=1, source_target_pairs={{0,4},{2,6},{4,0},{6,2},{8,12},{10,14},{12,8},{14,10},{16,20},{18,... | collective-permute-start | bytes 786440 | tf_op jit(solution)/shard_map/ppermute | solution.py:426
  50.9 1.2 %copy-start.2 = (bf16[256,2048]{1,0:T(8,128)(2,1)S(1)}, bf16[256,2048]{1,0:T(8,128)(2,1)}, u32[]{:S(2)}) copy-start(bf16[256,2048]{1,0:T(8,128)(2,1)} %refs_5_.5) | copy-start | bytes 3145732
  62.3 1.5 %copy-start = (f32[2,80,4096]{2,1,0:T(8,128)}, f32[2,80,4096]{2,1,0:T(8,128)S(1)}, u32[]{:S(2)}) copy-start(f32[2,80,4096]{2,1,0:T(8,128)S(1)} %doc_attention.4.refs_12_) | copy-start | bytes 7864324
  63.8 40.9 %copy-start.10 = (bf16[128,4096]{1,0:T(8,128)(2,1)S(1)}, bf16[128,4096]{1,0:T(8,128)(2,1)}, u32[]{:S(2)}) copy-start(bf16[128,4096]{1,0:T(8,128)(2,1)} %get-tuple-element.17) | copy-start | bytes 3145732
  101.7 6.4 %collective-permute-start.9 = (bf16[128,1024]{1,0:T(8,128)(2,1)S(1)}, bf16[128,1024]{1,0:T(8,128)(2,1)S(1)}, u32[]{:S(2)}, u32[]{:S(2)}) collective-permute-start(bf16[128,1024]{1,0:T(8,128)(2,1)S(1)} %get-tuple-element.25), channel_id=1, source_target_pairs={{0,1},{1,0},{2,3},{3,2},{4,5},{5,4},{6,7},{7,6},{8,9},{9,8},{10,11... | collective-permute-start | bytes 786440 | tf_op jit(solution)/shard_map/ppermute | solution.py:489
  102.0 6.9 %collective-permute-start.10 = (bf16[128,1024]{1,0:T(8,128)(2,1)S(1)}, bf16[128,1024]{1,0:T(8,128)(2,1)S(1)}, u32[]{:S(2)}, u32[]{:S(2)}) collective-permute-start(bf16[128,1024]{1,0:T(8,128)(2,1)S(1)} %get-tuple-element.26), channel_id=1, source_target_pairs={{0,2},{1,3},{2,0},{3,1},{4,6},{5,7},{6,4},{7,5},{8,10},{9,11},{10,... | collective-permute-start | bytes 786440 | tf_op jit(solution)/shard_map/ppermute | solution.py:489
  103.6 11.8 %collective-permute-start.11 = (bf16[128,1024]{1,0:T(8,128)(2,1)S(1)}, bf16[128,1024]{1,0:T(8,128)(2,1)S(1)}, u32[]{:S(2)}, u32[]{:S(2)}) collective-permute-start(bf16[128,1024]{1,0:T(8,128)(2,1)S(1)} %get-tuple-element.27), channel_id=1, source_target_pairs={{0,3},{1,2},{2,1},{3,0},{4,7},{5,6},{6,5},{7,4},{8,11},{9,10},{10,... | collective-permute-start | bytes 786440 | tf_op jit(solution)/shard_map/ppermute | solution.py:489
  105.8 10.3 %copy-start.11 = (bf16[128,4096]{1,0:T(8,128)(2,1)}, bf16[128,4096]{1,0:T(8,128)(2,1)S(1)}, u32[]{:S(2)}) copy-start(bf16[128,4096]{1,0:T(8,128)(2,1)S(1)} %constant_dynamic-update-slice_fusion.3) | copy-start | bytes 3145732
